TPU v7x, 1024 devices: a whole 4x4x32 slice. The times are simulated.
1024 devices in a mesh: row: 32 (over z), col: 32 (over x, y, core).
Axes of the slice: x: 4, y: 4, z: 32, core: 2. Of those that a mesh axis runs over, the one named last changes fastest.
Arguments:
- blocks: bfloat16 [2048, 8, 128, 128], P(('row', 'col')), may hold values from -1.5 to 1.5
- colidx: int32 [2048, 8], P(('row', 'col')), may hold values from 0 to 2047, as said below
- counts: int32 [32, 32], P('row', 'col'), may hold values from 1 to 66, as said below
- out_list: int32 [32, 32, 66], P('row', 'col'), may hold values from 0 to 65, as said below
Outputs:
- packed: bfloat16 [67584, 128, 128], P(('row', 'col'))
- offsets: int32 [32, 32], P('row', 'col')
Inputs may be any that keep to these rules, and one draw needn't show every extreme that they name: `colidx`: block row i names 8 distinct block columns (i + e) mod 2048 with -8 <= e <= 8; among them are i, (i - 8) mod 2048 and (i + 8) mod 2048. `counts`: some device keeps all 66 blocks and some device keeps one. `out_list`: each device's list is an ordering of 0 to 65; only its first counts entries are used.
All inputs are finite; a program needn't handle non-finite values.
Results may differ from a plain program's by a relative error of at most 0.001.
Values may be sent and summed in bfloat16 or wider, within the bound.
No kernel may reach another device: no remote copies, remote signals or barrier semaphores. Data moves between devices by JAX's collectives and lax.ppermute only.
A program may use at most 64 MiB of HBM per device.

v0:
```python
import jax
import jax.numpy as jnp
from jax import lax
from jax.sharding import PartitionSpec as P

H = 8


def shifted(x, axis, by):
    length = lax.axis_size(axis)
    return lax.ppermute(x, axis, [(i, (i + by) % length) for i in range(length)])


def carried_in(part, axis, combine, identity):
    place = lax.axis_index(axis)
    gathered = lax.all_gather(part, axis)
    state = jnp.zeros_like(part) + jnp.asarray(identity, part.dtype)

    def one(hop, state):
        return combine(state, lax.dynamic_index_in_dim(gathered, hop, 0, False))

    return lax.fori_loop(0, place, one, state)


def add_ints(earlier, later):
    return earlier + later


def shards(blocks, colidx, counts, out_list):
    rows_here = blocks.shape[0]
    slot_count = blocks.shape[1]
    block_size = blocks.shape[2]
    devices_all = lax.axis_size("row") * lax.axis_size("col")
    block_total = rows_here * devices_all
    device = lax.axis_index("row") * lax.axis_size("col") + lax.axis_index("col")
    first_row = device * rows_here
    side_count = (H + rows_here - 1) // rows_here
    below_pieces = []
    above_pieces = []
    lower_blocks, lower_cols = (blocks, colidx)
    upper_blocks, upper_cols = (blocks, colidx)
    for distance in range(side_count):
        lower_blocks, lower_cols = shifted((lower_blocks, lower_cols), ("row", "col"), 1)
        upper_blocks, upper_cols = shifted((upper_blocks, upper_cols), ("row", "col"), -1)
        below_pieces.append((lower_blocks, lower_cols))
        above_pieces.append((upper_blocks, upper_cols))
    ordered = list(reversed(below_pieces)) + [(blocks, colidx)] + above_pieces
    near_blocks = jnp.concatenate([piece[0] for piece in ordered], axis=0)
    near_cols = jnp.concatenate([piece[1] for piece in ordered], axis=0)
    band_size = 4 * H + 1
    row_ids = first_row + jnp.arange(rows_here, dtype=jnp.int32)
    row_range = jnp.arange(rows_here, dtype=jnp.int32)[:, None]
    local_place = (colidx - first_row + side_count * rows_here) % block_total

    def accumulate(slot_index, running):
        a_blocks = lax.dynamic_index_in_dim(blocks, slot_index, 1, keepdims=False)
        wanted = lax.dynamic_index_in_dim(local_place, slot_index, 1, keepdims=False)
        b_blocks = jnp.take(near_blocks, wanted, axis=0)
        b_cols = jnp.take(near_cols, wanted, axis=0)
        products = jnp.einsum(
            "iab,iubc->iuac", a_blocks, b_blocks, preferred_element_type=jnp.float32
        )
        places = (b_cols - row_ids[:, None] + 2 * H) % block_total
        return running.at[row_range, places].add(products)

    zero_tile = jnp.zeros((rows_here, band_size, block_size, block_size), jnp.float32)
    grid_tile = lax.fori_loop(0, slot_count, accumulate, zero_tile)
    tile_count = rows_here * band_size
    flattened = grid_tile.reshape(tile_count, block_size, block_size)
    picked = jnp.take(flattened, out_list[0, 0], axis=0)
    in_list = jnp.arange(tile_count, dtype=jnp.int32) < counts[0, 0]
    packed = jnp.where(in_list[:, None, None], picked, jnp.zeros_like(picked)).astype(jnp.bfloat16)
    zero_count = jnp.zeros((1, 1), jnp.int32)
    within = carried_in(counts, "col", add_ints, zero_count)
    row_sum = lax.psum(counts, "col")
    rows_before = carried_in(row_sum, "row", add_ints, zero_count)
    offsets = (rows_before + within).astype(jnp.int32)
    return (packed, offsets)


def solution(mesh):
    in_specs = (
        P(("row", "col"), None, None, None),
        P(("row", "col"), None),
        P("row", "col"),
        P("row", "col", None),
    )
    out_specs = (P(("row", "col"), None, None), P("row", "col"))
    return jax.shard_map(shards, mesh=mesh, in_specs=in_specs, out_specs=out_specs, check_vma=False)
```

profile of v0, /device:TPU:1, one launch (start us, length us, event | category | flops | bytes accessed | tf_op | source)
XLA Modules:
  0.0 314.0 jit_solution(10114155727706673333)
XLA Ops:
  0.6 4.7 %collective-permute-start.8 = (bf16[2,8,128,128]{3,2,1,0:T(8,128)(2,1)}, bf16[2,8,128,128]{3,2,1,0:T(8,128)(2,1)S(1)}, u32[]{:S(2)}, u32[]{:S(2)}) collective-permute-start(bf16[2,8,128,128]{3,2,1,0:T(8,128)(2,1)} %param.10), channel_id=1, source_target_pairs={{0,1},{1,2},{2,3},{3,4},{4,5},{5,6},{6,7},{7,8},{8,9},{9,10},{10,1... | collective-permute-start | bytes 1572872 | tf_op jit(solution)/shard_map/ppermute | solution.py:11
  5.4 13.4 %collective-permute-start.12 = (bf16[2,8,128,128]{3,2,1,0:T(8,128)(2,1)}, bf16[2,8,128,128]{3,2,1,0:T(8,128)(2,1)S(1)}, u32[]{:S(2)}, u32[]{:S(2)}) collective-permute-start(bf16[2,8,128,128]{3,2,1,0:T(8,128)(2,1)} %param.10), channel_id=1, source_target_pairs={{0,1023},{1,0},{2,1},{3,2},{4,3},{5,4},{6,5},{7,6},{8,7},{9,8},{10... | collective-permute-start | bytes 1572872 | tf_op jit(solution)/shard_map/ppermute | solution.py:11
  18.7 1.9 collective-permute-start.9
  20.7 15.3 %collective-permute-start.13 = (bf16[2,8,128,128]{3,2,1,0:T(8,128)(2,1)S(1)}, bf16[2,8,128,128]{3,2,1,0:T(8,128)(2,1)S(1)}, u32[]{:S(2)}, u32[]{:S(2)}) collective-permute-start(bf16[2,8,128,128]{3,2,1,0:T(8,128)(2,1)S(1)} %collective-permute-done.12), channel_id=1, source_target_pairs={{0,1023},{1,0},{2,1},{3,2},{4,3},{5,4},{6,5},{7,6},{8,7},{9,8},{10... | collective-permute-start | bytes 1572872 | tf_op jit(solution)/shard_map/ppermute | solution.py:11
  35.9 1.9 collective-permute-start.10
  37.9 0.8 copy.20
  38.6 1.9 collective-permute-start
  40.5 14.0 %collective-permute-start.4 = (s32[2,8]{0,1:T(8,128)S(1)}, s32[2,8]{0,1:T(8,128)S(1)}, u32[]{:S(2)}, u32[]{:S(2)}) collective-permute-start(s32[2,8]{0,1:T(8,128)S(1)} %copy.20), channel_id=1, source_target_pairs={{0,1023},{1,0},{2,1},{3,2},{4,3},{5,4},{6,5},{7,6},{8,7},{9,8},{10... | collective-permute-start | bytes 200 | tf_op jit(solution)/shard_map/ppermute | solution.py:11
  55.2 1.3 dynamic-slice.1
  56.4 0.7 bitcast_dynamic-update-slice_fusion
  57.1 10.0 %all-reduce.2 = (s32[1,1,1]{2,1,0:T(1,128)}, s32[32]{0:T(128)S(1)}) all-reduce(s32[1,1,1]{2,1,0:T(1,128)} %bitcast.7, s32[32]{0:T(128)S(1)} %bitcast_dynamic-update-slice_fusion), channel_id=1, replica_groups=mesh['row'=32,'col'=32] {'col'}, use_global_device_ids=true, to_apply=%region_3.4 | all-reduce | flops 33 | bytes 264 | tf_op jit(solution)/shard_map/psum | solution.py:75
  67.2 1.4 dynamic-slice
  68.5 1.3 bitcast_dynamic-update-slice_fusion.1
  69.9 30.7 %all-reduce = s32[32]{0:T(128)S(1)} all-reduce(s32[32]{0:T(128)S(1)} %bitcast_dynamic-update-slice_fusion.1), channel_id=1, replica_groups=mesh['row'=32,'col'=32] {'row'}, use_global_device_ids=true, to_apply=%add | all-reduce | flops 32 | bytes 256
  100.6 1.2 while.37
  100.6 0.6 constant_dynamic-slice_fusion.5
  101.8 0.7 fusion.18
  102.5 8.5 %collective-permute-start.14 = (bf16[2,8,128,128]{3,2,1,0:T(8,128)(2,1)S(1)}, bf16[2,8,128,128]{3,2,1,0:T(8,128)(2,1)}, u32[]{:S(2)}, u32[]{:S(2)}) collective-permute-start(bf16[2,8,128,128]{3,2,1,0:T(8,128)(2,1)S(1)} %collective-permute-done.13), channel_id=1, source_target_pairs={{0,1023},{1,0},{2,1},{3,2},{4,3},{5,4},{6,5},{7,6},{8,7},{9,8},{10... | collective-permute-start | bytes 1572872 | tf_op jit(solution)/shard_map/ppermute | solution.py:11
  111.0 4.2 %collective-permute-start.11 = (bf16[2,8,128,128]{3,2,1,0:T(8,128)(2,1)S(1)}, bf16[2,8,128,128]{3,2,1,0:T(8,128)(2,1)}, u32[]{:S(2)}, u32[]{:S(2)}) collective-permute-start(bf16[2,8,128,128]{3,2,1,0:T(8,128)(2,1)S(1)} %collective-permute-done.10), channel_id=1, source_target_pairs={{0,1},{1,2},{2,3},{3,4},{4,5},{5,6},{6,7},{7,8},{8,9},{9,10},{10,1... | collective-permute-start | bytes 1572872 | tf_op jit(solution)/shard_map/ppermute | solution.py:11
  115.3 0.7 compare_and_fusion
  116.0 2.4 collective-permute-start.1
  118.4 77.0 %collective-permute-start.5 = (s32[2,8]{0,1:T(8,128)S(1)}, s32[2,8]{0,1:T(8,128)S(1)}, u32[]{:S(2)}, u32[]{:S(2)}) collective-permute-start(s32[2,8]{0,1:T(8,128)S(1)} %collective-permute-done.4), channel_id=1, source_target_pairs={{0,1023},{1,0},{2,1},{3,2},{4,3},{5,4},{6,5},{7,6},{8,7},{9,8},{10... | collective-permute-start | bytes 200 | tf_op jit(solution)/shard_map/ppermute | solution.py:11
  195.4 1.9 collective-permute-start.2
  197.4 11.4 %collective-permute-start.6 = (s32[2,8]{0,1:T(8,128)S(1)}, s32[2,8]{0,1:T(8,128)S(1)}, u32[]{:S(2)}, u32[]{:S(2)}) collective-permute-start(s32[2,8]{0,1:T(8,128)S(1)} %collective-permute-done.5), channel_id=1, source_target_pairs={{0,1023},{1,0},{2,1},{3,2},{4,3},{5,4},{6,5},{7,6},{8,7},{9,8},{10... | collective-permute-start | bytes 200 | tf_op jit(solution)/shard_map/ppermute | solution.py:11
  208.8 1.9 collective-permute-start.3
  210.8 9.1 %collective-permute-start.7 = (s32[2,8]{0,1:T(8,128)S(1)}, s32[2,8]{0,1:T(8,128)S(1)}, u32[]{:S(2)}, u32[]{:S(2)}) collective-permute-start(s32[2,8]{0,1:T(8,128)S(1)} %collective-permute-done.6), channel_id=1, source_target_pairs={{0,1023},{1,0},{2,1},{3,2},{4,3},{5,4},{6,5},{7,6},{8,7},{9,8},{10... | collective-permute-start | bytes 200 | tf_op jit(solution)/shard_map/ppermute | solution.py:11
  219.8 0.8 collective-permute-done.7
  220.8 9.6 %collective-permute-start.15 = (bf16[2,8,128,128]{3,2,1,0:T(8,128)(2,1)}, bf16[2,8,128,128]{3,2,1,0:T(8,128)(2,1)S(1)}, u32[]{:S(2)}, u32[]{:S(2)}) collective-permute-start(bf16[2,8,128,128]{3,2,1,0:T(8,128)(2,1)} %collective-permute-done.14), channel_id=1, source_target_pairs={{0,1023},{1,0},{2,1},{3,2},{4,3},{5,4},{6,5},{7,6},{8,7},{9,8},{10... | collective-permute-start | bytes 1572872 | tf_op jit(solution)/shard_map/ppermute | solution.py:11
  230.4 1.9 constant_dynamic-update-slice_fusion.8
  232.3 0.8 constant_dynamic-update-slice_fusion.7
  233.1 0.9 constant_dynamic-update-slice_fusion.6
  234.0 0.8 constant_dynamic-update-slice_fusion.5
  234.8 0.8 constant_dynamic-update-slice_fusion.4
  235.7 0.8 constant_dynamic-update-slice_fusion.3
  236.5 0.8 constant_dynamic-update-slice_fusion.2
  237.3 1.9 constant_dynamic-update-slice_fusion.1
  239.2 0.8 constant_dynamic-update-slice_fusion
  240.1 2.6 broadcast_in_dim.86
  242.6 64.8 %while.38 = (s32[]{:T(128)}, f32[2,33,128,128]{3,2,1,0:T(8,128)}, s32[2,8]{0,1:T(8,128)S(1)}, s32[18,8]{1,0:T(8,128)S(1)}, bf16[18,8,128,128]{3,2,1,0:T(8,128)(2...) while((s32[]{:T(128)}, f32[2,33,128,128]{3,2,1,0:T(8,128)}, ...), condition=%wide.region_2.3_spmd.clone, body=%wide.region_0.2_spmd.clone.sunk | while | flops 67634568 | bytes 7935153 | solution.py:67
  242.7 0.6 gather_fusion
  243.4 3.0 gather_fusion.1
  247.2 3.6 %scatter_fusion = f32[2,33,128,128]{3,2,1,0:T(8,128)} fusion(f32[2,33,128,128]{3,2,1,0:T(8,128)} %get-tuple-element.461, s32[16]{0:T(128)S(1)} %reshape.250, f32[16,128,128]{2,1,0:T(8,128)S(1)} %copy.34), kind=kCustom, calls=%fused_computation.3.clone.clone.1 | custom fusion | flops 262144 | bytes 3145856 | tf_op jit(solution)/shard_map/while/body/eval_jaxpr/scatter-add | solution.py:64
  250.8 0.6 gather_fusion
  251.5 3.0 gather_fusion.1
  255.3 3.6 %scatter_fusion = f32[2,33,128,128]{3,2,1,0:T(8,128)} fusion(f32[2,33,128,128]{3,2,1,0:T(8,128)} %get-tuple-element.461, s32[16]{0:T(128)S(1)} %reshape.250, f32[16,128,128]{2,1,0:T(8,128)S(1)} %copy.34), kind=kCustom, calls=%fused_computation.3.clone.clone.1 | custom fusion | flops 262144 | bytes 3145856 | tf_op jit(solution)/shard_map/while/body/eval_jaxpr/scatter-add | solution.py:64
  258.9 0.6 gather_fusion
  259.6 3.0 gather_fusion.1
  263.4 3.6 %scatter_fusion = f32[2,33,128,128]{3,2,1,0:T(8,128)} fusion(f32[2,33,128,128]{3,2,1,0:T(8,128)} %get-tuple-element.461, s32[16]{0:T(128)S(1)} %reshape.250, f32[16,128,128]{2,1,0:T(8,128)S(1)} %copy.34), kind=kCustom, calls=%fused_computation.3.clone.clone.1 | custom fusion | flops 262144 | bytes 3145856 | tf_op jit(solution)/shard_map/while/body/eval_jaxpr/scatter-add | solution.py:64
  267.0 0.6 gather_fusion
  267.7 3.0 gather_fusion.1
  271.5 3.5 %scatter_fusion = f32[2,33,128,128]{3,2,1,0:T(8,128)} fusion(f32[2,33,128,128]{3,2,1,0:T(8,128)} %get-tuple-element.461, s32[16]{0:T(128)S(1)} %reshape.250, f32[16,128,128]{2,1,0:T(8,128)S(1)} %copy.34), kind=kCustom, calls=%fused_computation.3.clone.clone.1 | custom fusion | flops 262144 | bytes 3145856 | tf_op jit(solution)/shard_map/while/body/eval_jaxpr/scatter-add | solution.py:64
  275.1 0.6 gather_fusion
  275.8 3.0 gather_fusion.1
  279.6 3.6 %scatter_fusion = f32[2,33,128,128]{3,2,1,0:T(8,128)} fusion(f32[2,33,128,128]{3,2,1,0:T(8,128)} %get-tuple-element.461, s32[16]{0:T(128)S(1)} %reshape.250, f32[16,128,128]{2,1,0:T(8,128)S(1)} %copy.34), kind=kCustom, calls=%fused_computation.3.clone.clone.1 | custom fusion | flops 262144 | bytes 3145856 | tf_op jit(solution)/shard_map/while/body/eval_jaxpr/scatter-add | solution.py:64
  283.2 0.6 gather_fusion
  283.9 3.0 gather_fusion.1
  287.7 3.5 %scatter_fusion = f32[2,33,128,128]{3,2,1,0:T(8,128)} fusion(f32[2,33,128,128]{3,2,1,0:T(8,128)} %get-tuple-element.461, s32[16]{0:T(128)S(1)} %reshape.250, f32[16,128,128]{2,1,0:T(8,128)S(1)} %copy.34), kind=kCustom, calls=%fused_computation.3.clone.clone.1 | custom fusion | flops 262144 | bytes 3145856 | tf_op jit(solution)/shard_map/while/body/eval_jaxpr/scatter-add | solution.py:64
  291.3 0.6 gather_fusion
  292.0 3.0 gather_fusion.1
  295.8 3.5 %scatter_fusion = f32[2,33,128,128]{3,2,1,0:T(8,128)} fusion(f32[2,33,128,128]{3,2,1,0:T(8,128)} %get-tuple-element.461, s32[16]{0:T(128)S(1)} %reshape.250, f32[16,128,128]{2,1,0:T(8,128)S(1)} %copy.34), kind=kCustom, calls=%fused_computation.3.clone.clone.1 | custom fusion | flops 262144 | bytes 3145856 | tf_op jit(solution)/shard_map/while/body/eval_jaxpr/scatter-add | solution.py:64
  300.1 3.0 gather_fusion.1
  303.9 3.6 %scatter_fusion = f32[2,33,128,128]{3,2,1,0:T(8,128)} fusion(f32[2,33,128,128]{3,2,1,0:T(8,128)} %get-tuple-element.461, s32[16]{0:T(128)S(1)} %reshape.250, f32[16,128,128]{2,1,0:T(8,128)S(1)} %copy.34), kind=kCustom, calls=%fused_computation.3.clone.clone.1 | custom fusion | flops 262144 | bytes 3145856 | tf_op jit(solution)/shard_map/while/body/eval_jaxpr/scatter-add | solution.py:64
  307.5 3.4 %gather_fusion.2 = bf16[66,128,128]{2,1,0:T(8,128)(2,1)S(1)} fusion(f32[66,128,128]{2,1,0:T(8,128)} %bitcast.63, s32[1024]{0:T(1024)S(1)} %pad_clamp_fusion.1), kind=kCustom, calls=%fused_computation.2 | custom fusion | bytes 4325640 | tf_op jit(solution)/shard_map/jit(_take)/gather | solution.py:70
  310.8 2.0 select_convert_fusion
  (90 shorter events, 8.5 us)
Async XLA Ops:
  0.6 234.2 %copy-start = (bf16[2,8,128,128]{3,2,1,0:T(8,128)(2,1)S(1)}, bf16[2,8,128,128]{3,2,1,0:T(8,128)(2,1)}, u32[]{:S(2)}) copy-start(bf16[2,8,128,128]{3,2,1,0:T(8,128)(2,1)} %param.10) | copy-start | bytes 1572868
  0.6 18.1 %collective-permute-start.8 = (bf16[2,8,128,128]{3,2,1,0:T(8,128)(2,1)}, bf16[2,8,128,128]{3,2,1,0:T(8,128)(2,1)S(1)}, u32[]{:S(2)}, u32[]{:S(2)}) collective-permute-start(bf16[2,8,128,128]{3,2,1,0:T(8,128)(2,1)} %param.10), channel_id=1, source_target_pairs={{0,1},{1,2},{2,3},{3,4},{4,5},{5,6},{6,7},{7,8},{8,9},{9,10},{10,1... | collective-permute-start | bytes 1572872 | tf_op jit(solution)/shard_map/ppermute | solution.py:11
  5.4 15.3 %collective-permute-start.12 = (bf16[2,8,128,128]{3,2,1,0:T(8,128)(2,1)}, bf16[2,8,128,128]{3,2,1,0:T(8,128)(2,1)S(1)}, u32[]{:S(2)}, u32[]{:S(2)}) collective-permute-start(bf16[2,8,128,128]{3,2,1,0:T(8,128)(2,1)} %param.10), channel_id=1, source_target_pairs={{0,1023},{1,0},{2,1},{3,2},{4,3},{5,4},{6,5},{7,6},{8,7},{9,8},{10... | collective-permute-start | bytes 1572872 | tf_op jit(solution)/shard_map/ppermute | solution.py:11
  18.7 17.2 %collective-permute-start.9 = (bf16[2,8,128,128]{3,2,1,0:T(8,128)(2,1)S(1)}, bf16[2,8,128,128]{3,2,1,0:T(8,128)(2,1)S(1)}, u32[]{:S(2)}, u32[]{:S(2)}) collective-permute-start(bf16[2,8,128,128]{3,2,1,0:T(8,128)(2,1)S(1)} %collective-permute-done.8), channel_id=1, source_target_pairs={{0,1},{1,2},{2,3},{3,4},{4,5},{5,6},{6,7},{7,8},{8,9},{9,10},{10,1... | collective-permute-start | bytes 1572872 | tf_op jit(solution)/shard_map/ppermute | solution.py:11
  20.7 81.8 %collective-permute-start.13 = (bf16[2,8,128,128]{3,2,1,0:T(8,128)(2,1)S(1)}, bf16[2,8,128,128]{3,2,1,0:T(8,128)(2,1)S(1)}, u32[]{:S(2)}, u32[]{:S(2)}) collective-permute-start(bf16[2,8,128,128]{3,2,1,0:T(8,128)(2,1)S(1)} %collective-permute-done.12), channel_id=1, source_target_pairs={{0,1023},{1,0},{2,1},{3,2},{4,3},{5,4},{6,5},{7,6},{8,7},{9,8},{10... | collective-permute-start | bytes 1572872 | tf_op jit(solution)/shard_map/ppermute | solution.py:11
  35.9 75.1 %collective-permute-start.10 = (bf16[2,8,128,128]{3,2,1,0:T(8,128)(2,1)S(1)}, bf16[2,8,128,128]{3,2,1,0:T(8,128)(2,1)S(1)}, u32[]{:S(2)}, u32[]{:S(2)}) collective-permute-start(bf16[2,8,128,128]{3,2,1,0:T(8,128)(2,1)S(1)} %collective-permute-done.9), channel_id=1, source_target_pairs={{0,1},{1,2},{2,3},{3,4},{4,5},{5,6},{6,7},{7,8},{8,9},{9,10},{10,1... | collective-permute-start | bytes 1572872 | tf_op jit(solution)/shard_map/ppermute | solution.py:11
  38.6 77.3 %collective-permute-start = (s32[2,8]{0,1:T(8,128)S(1)}, s32[2,8]{0,1:T(8,128)S(1)}, u32[]{:S(2)}, u32[]{:S(2)}) collective-permute-start(s32[2,8]{0,1:T(8,128)S(1)} %copy.20), channel_id=1, source_target_pairs={{0,1},{1,2},{2,3},{3,4},{4,5},{5,6},{6,7},{7,8},{8,9},{9,10},{10,1... | collective-permute-start | bytes 200 | tf_op jit(solution)/shard_map/ppermute | solution.py:11
  40.5 77.8 %collective-permute-start.4 = (s32[2,8]{0,1:T(8,128)S(1)}, s32[2,8]{0,1:T(8,128)S(1)}, u32[]{:S(2)}, u32[]{:S(2)}) collective-permute-start(s32[2,8]{0,1:T(8,128)S(1)} %copy.20), channel_id=1, source_target_pairs={{0,1023},{1,0},{2,1},{3,2},{4,3},{5,4},{6,5},{7,6},{8,7},{9,8},{10... | collective-permute-start | bytes 200 | tf_op jit(solution)/shard_map/ppermute | solution.py:11
  102.5 118.3 %collective-permute-start.14 = (bf16[2,8,128,128]{3,2,1,0:T(8,128)(2,1)S(1)}, bf16[2,8,128,128]{3,2,1,0:T(8,128)(2,1)}, u32[]{:S(2)}, u32[]{:S(2)}) collective-permute-start(bf16[2,8,128,128]{3,2,1,0:T(8,128)(2,1)S(1)} %collective-permute-done.13), channel_id=1, source_target_pairs={{0,1023},{1,0},{2,1},{3,2},{4,3},{5,4},{6,5},{7,6},{8,7},{9,8},{10... | collective-permute-start | bytes 1572872 | tf_op jit(solution)/shard_map/ppermute | solution.py:11
  111.0 119.4 %collective-permute-start.11 = (bf16[2,8,128,128]{3,2,1,0:T(8,128)(2,1)S(1)}, bf16[2,8,128,128]{3,2,1,0:T(8,128)(2,1)}, u32[]{:S(2)}, u32[]{:S(2)}) collective-permute-start(bf16[2,8,128,128]{3,2,1,0:T(8,128)(2,1)S(1)} %collective-permute-done.10), channel_id=1, source_target_pairs={{0,1},{1,2},{2,3},{3,4},{4,5},{5,6},{6,7},{7,8},{8,9},{9,10},{10,1... | collective-permute-start | bytes 1572872 | tf_op jit(solution)/shard_map/ppermute | solution.py:11
  116.0 79.4 %collective-permute-start.1 = (s32[2,8]{0,1:T(8,128)S(1)}, s32[2,8]{0,1:T(8,128)S(1)}, u32[]{:S(2)}, u32[]{:S(2)}) collective-permute-start(s32[2,8]{0,1:T(8,128)S(1)} %collective-permute-done), channel_id=1, source_target_pairs={{0,1},{1,2},{2,3},{3,4},{4,5},{5,6},{6,7},{7,8},{8,9},{9,10},{10,1... | collective-permute-start | bytes 200 | tf_op jit(solution)/shard_map/ppermute | solution.py:11
  118.4 79.0 %collective-permute-start.5 = (s32[2,8]{0,1:T(8,128)S(1)}, s32[2,8]{0,1:T(8,128)S(1)}, u32[]{:S(2)}, u32[]{:S(2)}) collective-permute-start(s32[2,8]{0,1:T(8,128)S(1)} %collective-permute-done.4), channel_id=1, source_target_pairs={{0,1023},{1,0},{2,1},{3,2},{4,3},{5,4},{6,5},{7,6},{8,7},{9,8},{10... | collective-permute-start | bytes 200 | tf_op jit(solution)/shard_map/ppermute | solution.py:11
  195.4 13.4 %collective-permute-start.2 = (s32[2,8]{0,1:T(8,128)S(1)}, s32[2,8]{0,1:T(8,128)S(1)}, u32[]{:S(2)}, u32[]{:S(2)}) collective-permute-start(s32[2,8]{0,1:T(8,128)S(1)} %collective-permute-done.1), channel_id=1, source_target_pairs={{0,1},{1,2},{2,3},{3,4},{4,5},{5,6},{6,7},{7,8},{8,9},{9,10},{10,1... | collective-permute-start | bytes 200 | tf_op jit(solution)/shard_map/ppermute | solution.py:11
  197.4 13.4 %collective-permute-start.6 = (s32[2,8]{0,1:T(8,128)S(1)}, s32[2,8]{0,1:T(8,128)S(1)}, u32[]{:S(2)}, u32[]{:S(2)}) collective-permute-start(s32[2,8]{0,1:T(8,128)S(1)} %collective-permute-done.5), channel_id=1, source_target_pairs={{0,1023},{1,0},{2,1},{3,2},{4,3},{5,4},{6,5},{7,6},{8,7},{9,8},{10... | collective-permute-start | bytes 200 | tf_op jit(solution)/shard_map/ppermute | solution.py:11
  208.8 11.0 %collective-permute-start.3 = (s32[2,8]{0,1:T(8,128)S(1)}, s32[2,8]{0,1:T(8,128)S(1)}, u32[]{:S(2)}, u32[]{:S(2)}) collective-permute-start(s32[2,8]{0,1:T(8,128)S(1)} %collective-permute-done.2), channel_id=1, source_target_pairs={{0,1},{1,2},{2,3},{3,4},{4,5},{5,6},{6,7},{7,8},{8,9},{9,10},{10,1... | collective-permute-start | bytes 200 | tf_op jit(solution)/shard_map/ppermute | solution.py:11
  210.8 9.9 %collective-permute-start.7 = (s32[2,8]{0,1:T(8,128)S(1)}, s32[2,8]{0,1:T(8,128)S(1)}, u32[]{:S(2)}, u32[]{:S(2)}) collective-permute-start(s32[2,8]{0,1:T(8,128)S(1)} %collective-permute-done.6), channel_id=1, source_target_pairs={{0,1023},{1,0},{2,1},{3,2},{4,3},{5,4},{6,5},{7,6},{8,7},{9,8},{10... | collective-permute-start | bytes 200 | tf_op jit(solution)/shard_map/ppermute | solution.py:11
  220.8 18.4 %collective-permute-start.15 = (bf16[2,8,128,128]{3,2,1,0:T(8,128)(2,1)}, bf16[2,8,128,128]{3,2,1,0:T(8,128)(2,1)S(1)}, u32[]{:S(2)}, u32[]{:S(2)}) collective-permute-start(bf16[2,8,128,128]{3,2,1,0:T(8,128)(2,1)} %collective-permute-done.14), channel_id=1, source_target_pairs={{0,1023},{1,0},{2,1},{3,2},{4,3},{5,4},{6,5},{7,6},{8,7},{9,8},{10... | collective-permute-start | bytes 1572872 | tf_op jit(solution)/shard_map/ppermute | solution.py:11
where the time goes:
time: 316 us; the launch traced here: 314 us
  starting transfers between devices  179 us (57%)
  local copies, waits for them, and re-layouts  53.4 us (17%)
  blocking collectives  40.7 us (13%)
  other arithmetic  32.8 us (10%)
  matrix products  3.4 us (1%)
    ppermute x16, starting transfers between devices, shifted(): lax.ppermute(x, axis, [(i, (i + by) % length) for i in range(length)])  179 us
    unnamed x1, blocking collectives  30.7 us
    scatter-add x8, other arithmetic, accumulate(): return running.at[row_range, places].add(products)  28.4 us
    gather x8, local copies, waits for them, and re-layouts, accumulate(): b_blocks = jnp.take(near_blocks, wanted, axis=0)  23.9 us
    unnamed x18, local copies, waits for them, and re-layouts  14.3 us
    psum x1, blocking collectives, shards(): row_sum = lax.psum(counts, 'col')  10 us
  transfers between devices with their start and end apart: 16, of which 1 were waited for; matrix products, arithmetic and copies ran while one was open for 5% of the time, Pallas kernels for 0%

commit v1 on v0

v1 whole, which is shorter than its diff:
```python
import jax
import jax.numpy as jnp
from jax import lax
from jax.experimental import pallas as pl
from jax.experimental.pallas import tpu as pltpu
from jax.sharding import Mesh, PartitionSpec as P


H = 8
LANES = 128
META_ROWS = 16
ALL = ("row", "x", "y", "core")

OWN, I0, S1, S2, I1, I2, F1, I3, F2 = range(9)
SIDE_STEPS = {OWN: 0, I0: 1, S1: 2, S2: -2, I1: -1, I2: 3, F1: 4, I3: -3, F2: -4}


def chip_pairs(devices, step):
    return [(d, (d + 2 * (step if d % 2 == 0 else -step)) % devices) for d in range(devices)]


def core_pairs(devices):
    return [(d, d ^ 1) for d in range(devices)]


def far_pairs(rows, cols):
    return [(r * cols + c, (r + c) % rows * cols + c) for r in range(rows) for c in range(1, cols)]


def product_kernel(params, *refs):
    pieces = refs[:9]
    out = refs[9]
    near, acc, meta_vec, stage, meta, slot, load_sems, meta_sem, out_sems = refs[10:]
    tiles = acc.shape[0]
    band = tiles // 2
    size = acc.shape[1]
    slots = near.shape[1] // size // 2
    side = params[0]
    count = params[1]
    loads = []
    for p in range(9):
        copy = pltpu.make_async_copy(pieces[p], near.at[p], load_sems.at[p])
        copy.start()
        loads.append(copy)
    acc[...] = jnp.zeros_like(acc)

    @pl.loop(0, 2 * (2 * H + 2))
    def _(k):
        slot[k] = -1

    @pl.loop(0, 2 * slots)
    def _(k):
        a = k // slots
        slot[a * (2 * H + 2) + params[2 + k] + H + a] = k - a * slots

    first = 2 * slots * size
    for p in range(9):
        loads[p].wait()
        meta_vec[p:p + 1, :] = near[p, first:first + META_ROWS, :].astype(jnp.float32)[0:1, :].astype(jnp.int32)
    to_smem = pltpu.make_async_copy(meta_vec, meta, meta_sem)
    to_smem.start()
    to_smem.wait()
    for p in range(9):
        base = 2 * (SIDE_STEPS[p] * side + H // 2)

        @pl.loop(0, 4)
        def _(j):
            b = j // 2
            a = j - 2 * b
            rel = base + b
            t = slot[a * (2 * H + 2) + rel]

            @pl.when(t >= 0)
            def _():
                a_block = near[OWN, pl.ds(pl.multiple_of((a * slots + t) * size, size), size), :]
                shift = a * band + rel + H - a
                for u in range(0, slots, 2):
                    start = pl.multiple_of((b * slots + u) * size, size)
                    pair = jnp.concatenate(
                        [near[p, pl.ds(start, size), :], near[p, pl.ds(start + size, size), :]], axis=1
                    )
                    both = jnp.dot(a_block, pair, preferred_element_type=jnp.float32)
                    f = shift + meta[p, b * slots + u]
                    acc[f] = acc[f] + both[:, :size]
                    g = shift + meta[p, b * slots + u + 1]
                    acc[g] = acc[g] + both[:, size:]

    chunks = out_sems.shape[0]
    per = tiles // chunks
    stores = []
    for c in range(chunks):

        @pl.loop(c * per, (c + 1) * per)
        def _(p):
            @pl.when(p < count)
            def _():
                stage[p] = acc[params[2 + 2 * slots + p]].astype(stage.dtype)

            @pl.when(p >= count)
            def _():
                stage[p] = jnp.zeros((size, size), stage.dtype)

        copy = pltpu.make_async_copy(stage.at[pl.ds(c * per, per)], out.at[pl.ds(c * per, per)], out_sems.at[c])
        copy.start()
        stores.append(copy)
    for copy in stores:
        copy.wait()


def products(params, pieces, tiles, size):
    rows = pieces[0].shape[0]
    chunks = 6
    return pl.pallas_call(
        product_kernel,
        out_shape=jax.ShapeDtypeStruct((tiles, size, size), jnp.bfloat16),
        in_specs=[pl.BlockSpec(memory_space=pltpu.SMEM)] + [pl.BlockSpec(memory_space=pl.ANY)] * 9,
        out_specs=pl.BlockSpec(memory_space=pl.ANY),
        scratch_shapes=[
            pltpu.VMEM((9, rows, LANES), jnp.bfloat16),
            pltpu.VMEM((tiles, size, size), jnp.float32),
            pltpu.VMEM((16, LANES), jnp.int32),
            pltpu.VMEM((tiles, size, size), jnp.bfloat16),
            pltpu.SMEM((16, LANES), jnp.int32),
            pltpu.SMEM((64,), jnp.int32),
            pltpu.SemaphoreType.DMA((9,)),
            pltpu.SemaphoreType.DMA,
            pltpu.SemaphoreType.DMA((chunks,)),
        ],
        compiler_params=pltpu.CompilerParams(vmem_limit_bytes=24 * 1024 * 1024),
        cost_estimate=pl.CostEstimate(flops=600_000_000, bytes_accessed=8_000_000, transcendentals=0),
        name="products",
    )(params, *pieces)


def make_shards(shape):
    rows_of = shape["row"]
    cols_of = shape["x"] * shape["y"] * shape["core"]
    devices = rows_of * cols_of

    def compute(blocks, colidx, counts, out_list):
        here, slots, size = blocks.shape[:3]
        grid_row = lax.axis_index("row")
        col = lax.axis_index(("x", "y", "core"))
        device = grid_row * cols_of + col
        total = here * devices
        row_ids = device * here + jnp.arange(here, dtype=jnp.int32)[:, None]
        away = (colidx - row_ids + H) % total - H
        meta = jnp.zeros((META_ROWS, LANES), jnp.bfloat16).at[:, : here * slots].set(
            away.reshape(1, -1).astype(jnp.bfloat16)
        )
        own = jnp.concatenate([blocks.reshape(here * slots * size, size), meta], axis=0)

        def send(x, pairs):
            return lax.ppermute(x, ALL, pairs)

        down, up, swap = chip_pairs(devices, -1), chip_pairs(devices, 1), core_pairs(devices)
        s1 = send(own, down)
        s2 = send(own, up)
        f1 = send(s1, down)
        f2 = send(s2, up)
        i0 = send(own, swap)
        i1 = send(s1, swap)
        i2 = send(s2, swap)
        i3 = send(f1, swap)

        lane = jnp.arange(LANES, dtype=jnp.int32)
        kept = counts[0, 0]
        row_counts = jnp.where(lane == col, kept, 0)
        row_counts = lax.psum(row_counts, ("y", "core"))
        row_counts = lax.psum(row_counts, "x")
        within = jnp.sum(jnp.where(lane < col, row_counts, 0))
        row_total = jnp.broadcast_to(jnp.sum(row_counts), (LANES,))
        far = send(row_total, far_pairs(rows_of, cols_of))
        far, _ = lax.optimization_barrier((far, f1))
        before = jnp.where((col >= 1) & (col <= grid_row), far, 0)
        before = lax.psum(before, ("y", "core"))
        before = lax.psum(before, "x")
        offsets = (before[0] + within).astype(jnp.int32).reshape(1, 1)

        side = 1 - 2 * (col % 2)
        tiles = here * (4 * H + 1)
        params = jnp.concatenate(
            [side.reshape(1), counts.reshape(1), away.reshape(-1), out_list.reshape(-1)]
        ).astype(jnp.int32)
        by_name = {OWN: own, I0: i0, S1: s1, S2: s2, I1: i1, I2: i2, F1: f1, I3: i3, F2: f2}
        packed = products(params, [by_name[p] for p in range(9)], tiles, size)
        return (packed, offsets)

    return compute


def solution(mesh):
    rows_of, cols_of = mesh.shape["row"], mesh.shape["col"]
    fine = Mesh(mesh.devices.reshape(rows_of, cols_of // 8, 4, 2), ALL)
    col = ("x", "y", "core")
    in_specs = (
        P(ALL, None, None, None),
        P(ALL, None),
        P("row", col),
        P("row", col, None),
    )
    out_specs = (P(ALL, None, None), P("row", col))
    return jax.shard_map(
        make_shards(dict(fine.shape)), mesh=fine, in_specs=in_specs, out_specs=out_specs, check_vma=False
    )
```

time: 316 us -> 118 us (0.37)
  the two profiles are of different devices: /device:TPU:1 before, /device:TPU:24 now
where the time goes in v1:
time: 118 us
  blocking collectives  64.7 us (55%)
  starting transfers between devices  22.3 us (19%)
  waiting for transfers between devices  13.5 us (11%)
  Pallas kernels  9.34 us (8%)
  other arithmetic  3.91 us (3%)
  between operations  3.29 us (3%)
    psum x1, blocking collectives, compute(): row_counts = lax.psum(row_counts, ('y', 'core'))  32.3 us
    ppermute x9, starting transfers between devices, send(): return lax.ppermute(x, ALL, pairs)  22.3 us
    psum x1, blocking collectives, compute(): before = lax.psum(before, 'x')  18.8 us
    ppermute x9, waiting for transfers between devices, send(): return lax.ppermute(x, ALL, pairs)  13.5 us
    pallas_call x1, Pallas kernels, products(): pl.pallas_call(product_kernel, out_shape=jax.ShapeDtypeStruct((tiles, siz...  9.34 us
    psum x1, blocking collectives, compute(): before = lax.psum(before, ('y', 'core'))  7.86 us
    psum x1, blocking collectives, compute(): row_counts = lax.psum(row_counts, 'x')  5.76 us
  transfers between devices with their start and end apart: 9, of which 2 were waited for; matrix products, arithmetic and copies ran while one was open for 1% of the time, Pallas kernels for 0%

profile of v1, /device:TPU:24, one launch (start us, length us, event | category | flops | bytes accessed | tf_op | source)
XLA Modules:
  0.0 117.8 jit_solution(17846831216411391748)
XLA Ops:
  0.6 0.0 copy-start
  0.6 0.6 compare_reduce_fusion
  1.3 0.8 fusion
  2.0 0.1 reshape.61
  2.1 0.6 broadcast_select_fusion.1
  2.8 1.1 pad_maximum_fusion.refs_0_
  3.9 2.7 %collective-permute-start.1 = (bf16[2064,128]{1,0:T(8,128)(2,1)S(1)}, bf16[2064,128]{1,0:T(8,128)(2,1)S(1)}, u32[]{:S(2)}, u32[]{:S(2)}) collective-permute-start(bf16[2064,128]{1,0:T(8,128)(2,1)S(1)} %pad_maximum_fusion.refs_0_), channel_id=1, source_target_pairs={{0,1022},{1,3},{2,0},{3,5},{4,2},{5,7},{6,4},{7,9},{8,6},{9,11},{1... | collective-permute-start | bytes 1585160 | tf_op jit(solution)/shard_map/ppermute | solution.py:154
  6.5 5.3 %collective-permute-start.2 = (bf16[2064,128]{1,0:T(8,128)(2,1)S(1)}, bf16[2064,128]{1,0:T(8,128)(2,1)S(1)}, u32[]{:S(2)}, u32[]{:S(2)}) collective-permute-start(bf16[2064,128]{1,0:T(8,128)(2,1)S(1)} %pad_maximum_fusion.refs_0_), channel_id=1, source_target_pairs={{0,2},{1,1023},{2,4},{3,1},{4,6},{5,3},{6,8},{7,5},{8,10},{9,7},{1... | collective-permute-start | bytes 1585160 | tf_op jit(solution)/shard_map/ppermute | solution.py:154
  11.9 9.3 %collective-permute-done.1.refs_2_ = bf16[2064,128]{1,0:T(8,128)(2,1)S(1)} collective-permute-done((bf16[2064,128]{1,0:T(8,128)(2,1)S(1)}, bf16[2064,128]{1,0:T(8,128)(2,1)S(1)}, u32[]{:S(2)}, u32[]{:S(2)}) %collective-permute-start.1) | collective-permute-done | bytes 528416 | tf_op jit(solution)/shard_map/ppermute | solution.py:154
  21.1 1.9 %collective-permute-start.5 = (bf16[2064,128]{1,0:T(8,128)(2,1)S(1)}, bf16[2064,128]{1,0:T(8,128)(2,1)S(1)}, u32[]{:S(2)}, u32[]{:S(2)}) collective-permute-start(bf16[2064,128]{1,0:T(8,128)(2,1)S(1)} %collective-permute-done.1.refs_2_), channel_id=1, source_target_pairs={{0,1022},{1,3},{2,0},{3,5},{4,2},{5,7},{6,4},{7,9},{8,6},{9,11},{1... | collective-permute-start | bytes 1585160 | tf_op jit(solution)/shard_map/ppermute | solution.py:154
  23.7 32.3 %psum.28 = s32[128]{0:T(128)S(1)} all-reduce(s32[128]{0:T(128)S(1)} %compare_select_fusion.3), channel_id=1, replica_groups=mesh['row'=32,'x'=4,'y'=4,'core'=2] {'y','core'}, use_global_device_ids=true, to_apply=%region_1.2 | all-reduce | flops 128 | bytes 1024 | tf_op jit(solution)/shard_map/psum | solution.py:169
  56.0 5.8 %psum.29 = s32[128]{0:T(128)S(1)} all-reduce(s32[128]{0:T(128)S(1)} %psum.28), channel_id=1, replica_groups=mesh['row'=32,'x'=4,'y'=4,'core'=2] {'x'}, use_global_device_ids=true, to_apply=%region_2.3 | all-reduce | flops 128 | bytes 1024 | tf_op jit(solution)/shard_map/psum | solution.py:170
  61.8 0.7 fusion.2
  62.4 0.6 broadcast_in_dim.22
  63.1 1.9 %collective-permute-start.8 = (s32[128]{0:T(128)S(1)}, s32[128]{0:T(128)S(1)}, u32[]{:S(2)}, u32[]{:S(2)}) collective-permute-start(s32[128]{0:T(128)S(1)} %broadcast_in_dim.22), channel_id=1, source_target_pairs={{1,33},{2,66},{3,99},{4,132},{5,165},{6,198},{7,231},{8,264},{9,29... | collective-permute-start | bytes 1544 | tf_op jit(solution)/shard_map/ppermute | solution.py:154
  65.0 1.9 %collective-permute-start = (bf16[2064,128]{1,0:T(8,128)(2,1)S(1)}, bf16[2064,128]{1,0:T(8,128)(2,1)S(1)}, u32[]{:S(2)}, u32[]{:S(2)}) collective-permute-start(bf16[2064,128]{1,0:T(8,128)(2,1)S(1)} %pad_maximum_fusion.refs_0_), channel_id=1, source_target_pairs={{0,1},{1,0},{2,3},{3,2},{4,5},{5,4},{6,7},{7,6},{8,9},{9,8},{10,11... | collective-permute-start | bytes 1585160 | tf_op jit(solution)/shard_map/ppermute | solution.py:154
  67.0 0.0 collective-permute-done.2.refs_3_
  67.0 1.9 %collective-permute-start.7 = (bf16[2064,128]{1,0:T(8,128)(2,1)S(1)}, bf16[2064,128]{1,0:T(8,128)(2,1)S(1)}, u32[]{:S(2)}, u32[]{:S(2)}) collective-permute-start(bf16[2064,128]{1,0:T(8,128)(2,1)S(1)} %collective-permute-done.2.refs_3_), channel_id=1, source_target_pairs={{0,2},{1,1023},{2,4},{3,1},{4,6},{5,3},{6,8},{7,5},{8,10},{9,7},{1... | collective-permute-start | bytes 1585160 | tf_op jit(solution)/shard_map/ppermute | solution.py:154
  68.9 2.4 %collective-permute-start.4 = (bf16[2064,128]{1,0:T(8,128)(2,1)S(1)}, bf16[2064,128]{1,0:T(8,128)(2,1)}, u32[]{:S(2)}, u32[]{:S(2)}) collective-permute-start(bf16[2064,128]{1,0:T(8,128)(2,1)S(1)} %collective-permute-done.2.refs_3_), channel_id=1, source_target_pairs={{0,1},{1,0},{2,3},{3,2},{4,5},{5,4},{6,7},{7,6},{8,9},{9,8},{10,11... | collective-permute-start | bytes 1585160 | tf_op jit(solution)/shard_map/ppermute | solution.py:154
  71.3 4.2 %collective-permute-done.8 = s32[128]{0:T(128)S(1)} collective-permute-done((s32[128]{0:T(128)S(1)}, s32[128]{0:T(128)S(1)}, u32[]{:S(2)}, u32[]{:S(2)}) %collective-permute-start.8) | collective-permute-done | bytes 544 | tf_op jit(solution)/shard_map/ppermute | solution.py:154
  75.5 1.9 %collective-permute-start.3 = (bf16[2064,128]{1,0:T(8,128)(2,1)S(1)}, bf16[2064,128]{1,0:T(8,128)(2,1)}, u32[]{:S(2)}, u32[]{:S(2)}) collective-permute-start(bf16[2064,128]{1,0:T(8,128)(2,1)S(1)} %collective-permute-done.1.refs_2_), channel_id=1, source_target_pairs={{0,1},{1,0},{2,3},{3,2},{4,5},{5,4},{6,7},{7,6},{8,9},{9,8},{10,11... | collective-permute-start | bytes 1585160 | tf_op jit(solution)/shard_map/ppermute | solution.py:154
  77.4 0.0 collective-permute-done.5.refs_6_
  77.4 2.4 %collective-permute-start.6 = (bf16[2064,128]{1,0:T(8,128)(2,1)S(1)}, bf16[2064,128]{1,0:T(8,128)(2,1)}, u32[]{:S(2)}, u32[]{:S(2)}) collective-permute-start(bf16[2064,128]{1,0:T(8,128)(2,1)S(1)} %collective-permute-done.5.refs_6_), channel_id=1, source_target_pairs={{0,1},{1,0},{2,3},{3,2},{4,5},{5,4},{6,7},{7,6},{8,9},{9,8},{10,11... | collective-permute-start | bytes 1585160 | tf_op jit(solution)/shard_map/ppermute | solution.py:154
  79.8 0.0 copy-done
  79.9 0.1 pad_add_fusion.params
  79.9 7.9 %psum.30 = s32[128]{0:T(128)S(1)} all-reduce(s32[128]{0:T(128)S(1)} %broadcast_select_fusion), channel_id=1, replica_groups=mesh['row'=32,'x'=4,'y'=4,'core'=2] {'y','core'}, use_global_device_ids=true, to_apply=%region_4.5 | all-reduce | flops 128 | bytes 1024 | tf_op jit(solution)/shard_map/psum | solution.py:176
  87.8 18.8 %psum.31 = s32[128]{0:T(128)S(1)} all-reduce(s32[128]{0:T(128)S(1)} %psum.30), channel_id=1, replica_groups=mesh['row'=32,'x'=4,'y'=4,'core'=2] {'x'}, use_global_device_ids=true, to_apply=%region_5.6 | all-reduce | flops 128 | bytes 1024 | tf_op jit(solution)/shard_map/psum | solution.py:177
  107.3 0.0 collective-permute-done.refs_1_
  107.3 0.0 collective-permute-done.7.refs_8_
  107.3 0.0 collective-permute-done.4.refs_5_
  107.3 0.0 collective-permute-done.3.refs_4_
  107.3 0.0 collective-permute-done.6.refs_7_
  107.3 9.3 %products.1 = bf16[66,128,128]{2,1,0:T(8,128)(2,1)} custom-call(s32[84]{0:T(128)S(1)} %pad_add_fusion.params, bf16[2064,128]{1,0:T(8,128)(2,1)S(1)} %pad_maximum_fusion.refs_0_, bf16[2064,128]{1,0:T(8,128)(2,1)S(1)} %collective-permute-done.refs_1_, bf16[2064,128]{1,0:T(8,128)(2,1)S(1)} %collective-permute-done.1.refs_2_, ...), custom_call_target="tpu_custom_call" | custom-call | flops 600000000 | bytes 8000000 | tf_op jit(solution)/shard_map/products/pallas_call | solution.py:113
  (5 shorter events, 0.0 us)
Async XLA Ops:
  0.6 79.2 %copy-start = (s32[1,1,66]{2,1,0:T(1,128)S(1)}, s32[1,1,66]{2,1,0:T(1,128)}, u32[]{:S(2)}) copy-start(s32[1,1,66]{2,1,0:T(1,128)} %param.9) | copy-start | bytes 796
  3.9 17.2 %collective-permute-start.1 = (bf16[2064,128]{1,0:T(8,128)(2,1)S(1)}, bf16[2064,128]{1,0:T(8,128)(2,1)S(1)}, u32[]{:S(2)}, u32[]{:S(2)}) collective-permute-start(bf16[2064,128]{1,0:T(8,128)(2,1)S(1)} %pad_maximum_fusion.refs_0_), channel_id=1, source_target_pairs={{0,1022},{1,3},{2,0},{3,5},{4,2},{5,7},{6,4},{7,9},{8,6},{9,11},{1... | collective-permute-start | bytes 1585160 | tf_op jit(solution)/shard_map/ppermute | solution.py:154
  6.5 60.4 %collective-permute-start.2 = (bf16[2064,128]{1,0:T(8,128)(2,1)S(1)}, bf16[2064,128]{1,0:T(8,128)(2,1)S(1)}, u32[]{:S(2)}, u32[]{:S(2)}) collective-permute-start(bf16[2064,128]{1,0:T(8,128)(2,1)S(1)} %pad_maximum_fusion.refs_0_), channel_id=1, source_target_pairs={{0,2},{1,1023},{2,4},{3,1},{4,6},{5,3},{6,8},{7,5},{8,10},{9,7},{1... | collective-permute-start | bytes 1585160 | tf_op jit(solution)/shard_map/ppermute | solution.py:154
  21.1 56.3 %collective-permute-start.5 = (bf16[2064,128]{1,0:T(8,128)(2,1)S(1)}, bf16[2064,128]{1,0:T(8,128)(2,1)S(1)}, u32[]{:S(2)}, u32[]{:S(2)}) collective-permute-start(bf16[2064,128]{1,0:T(8,128)(2,1)S(1)} %collective-permute-done.1.refs_2_), channel_id=1, source_target_pairs={{0,1022},{1,3},{2,0},{3,5},{4,2},{5,7},{6,4},{7,9},{8,6},{9,11},{1... | collective-permute-start | bytes 1585160 | tf_op jit(solution)/shard_map/ppermute | solution.py:154
  63.1 12.4 %collective-permute-start.8 = (s32[128]{0:T(128)S(1)}, s32[128]{0:T(128)S(1)}, u32[]{:S(2)}, u32[]{:S(2)}) collective-permute-start(s32[128]{0:T(128)S(1)} %broadcast_in_dim.22), channel_id=1, source_target_pairs={{1,33},{2,66},{3,99},{4,132},{5,165},{6,198},{7,231},{8,264},{9,29... | collective-permute-start | bytes 1544 | tf_op jit(solution)/shard_map/ppermute | solution.py:154
  65.0 42.2 %collective-permute-start = (bf16[2064,128]{1,0:T(8,128)(2,1)S(1)}, bf16[2064,128]{1,0:T(8,128)(2,1)S(1)}, u32[]{:S(2)}, u32[]{:S(2)}) collective-permute-start(bf16[2064,128]{1,0:T(8,128)(2,1)S(1)} %pad_maximum_fusion.refs_0_), channel_id=1, source_target_pairs={{0,1},{1,0},{2,3},{3,2},{4,5},{5,4},{6,7},{7,6},{8,9},{9,8},{10,11... | collective-permute-start | bytes 1585160 | tf_op jit(solution)/shard_map/ppermute | solution.py:154
  67.0 40.3 %collective-permute-start.7 = (bf16[2064,128]{1,0:T(8,128)(2,1)S(1)}, bf16[2064,128]{1,0:T(8,128)(2,1)S(1)}, u32[]{:S(2)}, u32[]{:S(2)}) collective-permute-start(bf16[2064,128]{1,0:T(8,128)(2,1)S(1)} %collective-permute-done.2.refs_3_), channel_id=1, source_target_pairs={{0,2},{1,1023},{2,4},{3,1},{4,6},{5,3},{6,8},{7,5},{8,10},{9,7},{1... | collective-permute-start | bytes 1585160 | tf_op jit(solution)/shard_map/ppermute | solution.py:154
  68.9 38.4 %collective-permute-start.4 = (bf16[2064,128]{1,0:T(8,128)(2,1)S(1)}, bf16[2064,128]{1,0:T(8,128)(2,1)}, u32[]{:S(2)}, u32[]{:S(2)}) collective-permute-start(bf16[2064,128]{1,0:T(8,128)(2,1)S(1)} %collective-permute-done.2.refs_3_), channel_id=1, source_target_pairs={{0,1},{1,0},{2,3},{3,2},{4,5},{5,4},{6,7},{7,6},{8,9},{9,8},{10,11... | collective-permute-start | bytes 1585160 | tf_op jit(solution)/shard_map/ppermute | solution.py:154
  75.5 31.8 %collective-permute-start.3 = (bf16[2064,128]{1,0:T(8,128)(2,1)S(1)}, bf16[2064,128]{1,0:T(8,128)(2,1)}, u32[]{:S(2)}, u32[]{:S(2)}) collective-permute-start(bf16[2064,128]{1,0:T(8,128)(2,1)S(1)} %collective-permute-done.1.refs_2_), channel_id=1, source_target_pairs={{0,1},{1,0},{2,3},{3,2},{4,5},{5,4},{6,7},{7,6},{8,9},{9,8},{10,11... | collective-permute-start | bytes 1585160 | tf_op jit(solution)/shard_map/ppermute | solution.py:154
  77.4 29.9 %collective-permute-start.6 = (bf16[2064,128]{1,0:T(8,128)(2,1)S(1)}, bf16[2064,128]{1,0:T(8,128)(2,1)}, u32[]{:S(2)}, u32[]{:S(2)}) collective-permute-start(bf16[2064,128]{1,0:T(8,128)(2,1)S(1)} %collective-permute-done.5.refs_6_), channel_id=1, source_target_pairs={{0,1},{1,0},{2,3},{3,2},{4,5},{5,4},{6,7},{7,6},{8,9},{9,8},{10,11... | collective-permute-start | bytes 1585160 | tf_op jit(solution)/shard_map/ppermute | solution.py:154

commit v2 on v1

v2 whole, which is shorter than its diff:
```python
import functools

import jax
import jax.numpy as jnp
from jax import lax
from jax.experimental import pallas as pl
from jax.experimental.pallas import tpu as pltpu
from jax.sharding import Mesh, PartitionSpec as P


H = 8
LANES = 128
META_ROWS = 16
VMEM_GRANT = 58 * 1024 * 1024
ALL = ("row", "x", "y", "core")

OWN, I0, S1, S2, I1, I2, F1, I3, F2 = range(9)
SIDE_STEPS = {OWN: 0, I0: 1, S1: 2, S2: -2, I1: -1, I2: 3, F1: 4, I3: -3, F2: -4}


def chip_pairs(devices, step):
    return [(d, (d + 2 * (step if d % 2 == 0 else -step)) % devices) for d in range(devices)]


def core_pairs(devices):
    return [(d, d ^ 1) for d in range(devices)]


def far_pairs(rows, cols):
    return [(r * cols + c, (r + c) % rows * cols + c) for r in range(rows) for c in range(1, cols)]


def build_slots(params, slot, slots):
    reach = 2 * H + 2

    @pl.loop(0, 2 * reach)
    def _(k):
        slot[k] = -1

    @pl.loop(0, 2 * slots)
    def _(k):
        a = k // slots
        slot[a * reach + params[2 + k] + H + a] = k - a * slots


def add_products(p, kind, side, own, piece, acc, slot, meta, slots):
    size = acc.shape[1]
    band = acc.shape[0] // 2
    base = 2 * (SIDE_STEPS[kind] * side + H // 2)

    @pl.loop(0, 4)
    def _(j):
        b = j // 2
        a = j - 2 * b
        rel = base + b
        t = slot[a * (2 * H + 2) + rel]

        @pl.when(t >= 0)
        def _():
            a_block = own[pl.ds(pl.multiple_of((a * slots + t) * size, size), size), :]
            shift = a * band + rel + H - a
            for u in range(0, slots, 2):
                start = pl.multiple_of((b * slots + u) * size, size)
                pair = jnp.concatenate(
                    [piece[pl.ds(start, size), :], piece[pl.ds(start + size, size), :]], axis=1
                )
                both = jnp.dot(a_block, pair, preferred_element_type=jnp.float32)
                f = shift + meta[2 * p + b, u]
                acc[f] = acc[f] + both[:, :size]
                g = shift + meta[2 * p + b, u + 1]
                acc[g] = acc[g] + both[:, size:]


def load_pieces(pieces, near, meta_raw, load_sems, meta_sems):
    metas = []
    loads = []
    for p, piece in enumerate(pieces):
        rows = piece.shape[0] - META_ROWS
        copy = pltpu.make_async_copy(piece.at[pl.ds(rows, META_ROWS)], meta_raw.at[p], meta_sems.at[p])
        copy.start()
        metas.append(copy)
    for p, piece in enumerate(pieces):
        rows = piece.shape[0] - META_ROWS
        copy = pltpu.make_async_copy(piece.at[pl.ds(0, rows)], near.at[p], load_sems.at[p])
        copy.start()
        loads.append(copy)
    return metas, loads


def read_meta(metas, meta_raw, meta_vec, meta, sem):
    for p, copy in enumerate(metas):
        copy.wait()
        meta_vec[2 * p:2 * p + 2, :] = meta_raw[p].astype(jnp.float32)[0:2, :].astype(jnp.int32)
    copy = pltpu.make_async_copy(meta_vec, meta, sem)
    copy.start()
    return copy


def early_kernel(kinds, slots, params, *refs):
    n = len(kinds)
    pieces = refs[:n]
    acc_out, near, acc, meta_raw, meta_vec, meta, slot, load_sems, meta_sems, sem, acc_sem = refs[n:]
    metas, loads = load_pieces(pieces, near, meta_raw, load_sems, meta_sems)
    copy = read_meta(metas, meta_raw, meta_vec, meta, sem)
    build_slots(params, slot, slots)
    acc[...] = jnp.zeros_like(acc)
    copy.wait()
    for p, kind in enumerate(kinds):
        loads[p].wait()
        add_products(p, kind, params[0], near.at[0], near.at[p], acc, slot, meta, slots)
    save = pltpu.make_async_copy(acc, acc_out, acc_sem)
    save.start()
    save.wait()


def late_kernel(kinds, slots, params, own, acc_in, *refs):
    n = len(kinds)
    pieces = refs[:n]
    out, a_rows, near, acc, meta_raw, meta_vec, stage, meta, slot = refs[n:n + 9]
    load_sems, meta_sems, sem, own_sem, acc_sem, out_sems = refs[n + 9:]
    tiles, size = acc.shape[:2]
    own_load = pltpu.make_async_copy(own.at[pl.ds(0, 2 * slots * size)], a_rows, own_sem)
    own_load.start()
    load = pltpu.make_async_copy(acc_in, acc, acc_sem)
    load.start()
    metas, loads = load_pieces(pieces, near, meta_raw, load_sems, meta_sems)
    copy = read_meta(metas, meta_raw, meta_vec, meta, sem)
    build_slots(params, slot, slots)
    copy.wait()
    own_load.wait()
    load.wait()
    for p, kind in enumerate(kinds):
        loads[p].wait()
        add_products(p, kind, params[0], a_rows, near.at[p], acc, slot, meta, slots)
    count = params[1]
    chunks = out_sems.shape[0]
    per = tiles // chunks
    stores = []
    for c in range(chunks):

        @pl.loop(c * per, (c + 1) * per)
        def _(p):
            @pl.when(p < count)
            def _():
                stage[p] = acc[params[2 + 2 * slots + p]].astype(stage.dtype)

            @pl.when(p >= count)
            def _():
                stage[p] = jnp.zeros((size, size), stage.dtype)

        copy = pltpu.make_async_copy(stage.at[pl.ds(c * per, per)], out.at[pl.ds(c * per, per)], out_sems.at[c])
        copy.start()
        stores.append(copy)
    for copy in stores:
        copy.wait()


def scratch(n, tiles, size, slots):
    return [
        pltpu.VMEM((n, 2 * slots * size, size), jnp.bfloat16),
        pltpu.VMEM((tiles, size, size), jnp.float32),
        pltpu.VMEM((n, META_ROWS, LANES), jnp.bfloat16),
        pltpu.VMEM((16, LANES), jnp.int32),
    ]


def early_products(params, kinds, pieces, tiles, size, slots):
    n = len(kinds)
    return pl.pallas_call(
        functools.partial(early_kernel, kinds, slots),
        out_shape=jax.ShapeDtypeStruct((tiles, size, size), jnp.float32),
        in_specs=[pl.BlockSpec(memory_space=pltpu.SMEM)] + [pl.BlockSpec(memory_space=pl.ANY)] * n,
        out_specs=pl.BlockSpec(memory_space=pl.ANY),
        scratch_shapes=scratch(n, tiles, size, slots)
        + [
            pltpu.SMEM((16, LANES), jnp.int32),
            pltpu.SMEM((64,), jnp.int32),
            pltpu.SemaphoreType.DMA((n,)),
            pltpu.SemaphoreType.DMA((n,)),
            pltpu.SemaphoreType.DMA,
            pltpu.SemaphoreType.DMA,
        ],
        compiler_params=pltpu.CompilerParams(vmem_limit_bytes=VMEM_GRANT),
        cost_estimate=pl.CostEstimate(flops=300_000_000, bytes_accessed=4_000_000, transcendentals=0),
        name="early",
    )(params, *pieces)


def late_products(params, own, acc, kinds, pieces, slots):
    tiles, size = acc.shape[:2]
    n = len(kinds)
    chunks = 6
    return pl.pallas_call(
        functools.partial(late_kernel, kinds, slots),
        out_shape=jax.ShapeDtypeStruct((tiles, size, size), jnp.bfloat16),
        in_specs=[pl.BlockSpec(memory_space=pltpu.SMEM)] + [pl.BlockSpec(memory_space=pl.ANY)] * (n + 2),
        out_specs=pl.BlockSpec(memory_space=pl.ANY),
        scratch_shapes=[pltpu.VMEM((2 * slots * size, size), jnp.bfloat16)]
        + scratch(n, tiles, size, slots)
        + [
            pltpu.VMEM((tiles, size, size), jnp.bfloat16),
            pltpu.SMEM((16, LANES), jnp.int32),
            pltpu.SMEM((64,), jnp.int32),
            pltpu.SemaphoreType.DMA((n,)),
            pltpu.SemaphoreType.DMA((n,)),
            pltpu.SemaphoreType.DMA,
            pltpu.SemaphoreType.DMA,
            pltpu.SemaphoreType.DMA,
            pltpu.SemaphoreType.DMA((chunks,)),
        ],
        compiler_params=pltpu.CompilerParams(vmem_limit_bytes=VMEM_GRANT),
        cost_estimate=pl.CostEstimate(flops=300_000_000, bytes_accessed=6_000_000, transcendentals=0),
        name="late",
    )(params, own, acc, *pieces)


def make_shards(shape):
    rows_of = shape["row"]
    cols_of = shape["x"] * shape["y"] * shape["core"]
    devices = rows_of * cols_of

    def compute(blocks, colidx, counts, out_list):
        here, slots, size = blocks.shape[:3]
        grid_row = lax.axis_index("row")
        col = lax.axis_index(("x", "y", "core"))
        device = grid_row * cols_of + col
        total = here * devices
        row_ids = device * here + jnp.arange(here, dtype=jnp.int32)[:, None]
        away = colidx - row_ids
        away = jnp.where(away > H, away - total, jnp.where(away < -H, away + total, away))
        meta = jnp.pad(away.astype(jnp.bfloat16), ((0, META_ROWS - here), (0, LANES - slots)))
        own = jnp.concatenate([blocks.reshape(here * slots * size, size), meta], axis=0)

        def send(x, pairs):
            return lax.ppermute(x, ALL, pairs)

        down, up, swap = chip_pairs(devices, -1), chip_pairs(devices, 1), core_pairs(devices)
        s1 = send(own, down)
        s2 = send(own, up)
        f1 = send(s1, down)
        f2 = send(s2, up)
        i0 = send(own, swap)
        i1 = send(s1, swap)
        i2 = send(s2, swap)
        i3 = send(f1, swap)

        lane = jnp.arange(LANES, dtype=jnp.int32)
        kept = counts[0, 0]
        row_counts = jnp.where(lane == col, kept, 0)
        row_counts = lax.psum(row_counts, "x")
        row_counts = lax.psum(row_counts, ("y", "core"))
        within = jnp.sum(jnp.where(lane < col, row_counts, 0))
        row_total = jnp.broadcast_to(jnp.sum(row_counts), (LANES,))
        far = send(row_total, far_pairs(rows_of, cols_of))
        before = jnp.where((col >= 1) & (col <= grid_row), far, 0)
        before = lax.psum(before, "x")
        before = lax.psum(before, ("y", "core"))
        offsets = (before[0] + within).astype(jnp.int32).reshape(1, 1)

        side = 1 - 2 * (col % 2)
        tiles = here * (4 * H + 1)
        params = jnp.concatenate(
            [side.reshape(1), counts.reshape(1), away.reshape(-1), out_list.reshape(-1)]
        ).astype(jnp.int32)
        acc = early_products(params, (OWN, I0, S1, I1), (own, i0, s1, i1), tiles, size, slots)
        packed = late_products(params, own, acc, (S2, I2, F1, I3, F2), (s2, i2, f1, i3, f2), slots)
        return (packed, offsets)

    return compute


def solution(mesh):
    rows_of, cols_of = mesh.shape["row"], mesh.shape["col"]
    fine = Mesh(mesh.devices.reshape(rows_of, cols_of // 8, 4, 2), ALL)
    col = ("x", "y", "core")
    in_specs = (
        P(ALL, None, None, None),
        P(ALL, None),
        P("row", col),
        P("row", col, None),
    )
    out_specs = (P(ALL, None, None), P("row", col))
    return jax.shard_map(
        make_shards(dict(fine.shape)), mesh=fine, in_specs=in_specs, out_specs=out_specs, check_vma=False
    )
```

time: 118 us -> 129 us (1.093)
  Pallas kernels: 9.34 us -> 15.3 us
  waiting for transfers between devices: 13.5 us -> 17.8 us
  local copies, waits for them, and re-layouts: 0.74 us -> 2.36 us
    pallas_call x1 -> x2, Pallas kernels: 9.34 us -> 15.3 us  [the longest x1 8.73 us: late_products(): pl.pallas_call(functools.partial(late_kernel, kinds, slots), out_shape=ja...]
    psum x1, blocking collectives: 18.8 us -> 13.1 us  [compute(): before = lax.psum(before, 'x')]
    psum x1, blocking collectives: 7.86 us -> 13.6 us  [compute(): before = lax.psum(before, ('y', 'core'))]
    ppermute x9, waiting for transfers between devices: 13.5 us -> 17.8 us  [send(): return lax.ppermute(x, ALL, pairs)]
    psum x1, blocking collectives: 5.76 us -> 9.87 us  [compute(): row_counts = lax.psum(row_counts, 'x')]
    psum x1, blocking collectives: 32.3 us -> 28.2 us  [compute(): row_counts = lax.psum(row_counts, ('y', 'core'))]
    unnamed x2 -> x14, local copies, waits for them, and re-layouts: 0.01 us -> 1.64 us
  transfers between devices with their start and end apart: 9 -> 9, of which waited for: 2 -> 2; matrix products, arithmetic and copies ran while one was open for 1% -> 2% of each run, Pallas kernels for 0% -> 5%
where the time goes in v2:
time: 129 us
  blocking collectives  64.7 us (50%)
  starting transfers between devices  21.8 us (17%)
  waiting for transfers between devices  17.8 us (14%)
  Pallas kernels  15.3 us (12%)
  between operations  3.4 us (3%)
  other arithmetic  3.12 us (2%)
  local copies, waits for them, and re-layouts  2.36 us (2%)
    psum x1, blocking collectives, compute(): row_counts = lax.psum(row_counts, ('y', 'core'))  28.2 us
    ppermute x9, starting transfers between devices, send(): return lax.ppermute(x, ALL, pairs)  21.8 us
    ppermute x9, waiting for transfers between devices, send(): return lax.ppermute(x, ALL, pairs)  17.8 us
    psum x1, blocking collectives, compute(): before = lax.psum(before, ('y', 'core'))  13.6 us
    psum x1, blocking collectives, compute(): before = lax.psum(before, 'x')  13.1 us
    psum x1, blocking collectives, compute(): row_counts = lax.psum(row_counts, 'x')  9.87 us
    pallas_call x1, Pallas kernels, late_products(): pl.pallas_call(functools.partial(late_kernel, kinds, slots), out_shape=ja...  8.73 us
    pallas_call x1, Pallas kernels, early_products(): pl.pallas_call(functools.partial(early_kernel, kinds, slots), out_shape=j...  6.61 us
  transfers between devices with their start and end apart: 9, of which 2 were waited for; matrix products, arithmetic and copies ran while one was open for 2% of the time, Pallas kernels for 5%

profile of v2, /device:TPU:24, one launch (start us, length us, event | category | flops | bytes accessed | tf_op | source)
XLA Modules:
  0.0 128.6 jit_solution(2336042005681157991)
XLA Ops:
  0.6 0.0 copy-start.6
  0.7 0.8 fusion.3
  1.4 1.1 fusion.1.refs_0_.own
  2.5 0.0 copy-start
  2.5 2.7 %collective-permute-start.1 = (bf16[2064,128]{1,0:T(8,128)(2,1)S(1)}, bf16[2064,128]{1,0:T(8,128)(2,1)S(1)}, u32[]{:S(2)}, u32[]{:S(2)}) collective-permute-start(bf16[2064,128]{1,0:T(8,128)(2,1)S(1)} %fusion.1.refs_0_.own), channel_id=1, source_target_pairs={{0,1022},{1,3},{2,0},{3,5},{4,2},{5,7},{6,4},{7,9},{8,6},{9,11},{1... | collective-permute-start | bytes 1585160 | tf_op jit(solution)/shard_map/ppermute | solution.py:235
  5.2 5.3 %collective-permute-start.3 = (bf16[2064,128]{1,0:T(8,128)(2,1)S(1)}, bf16[2064,128]{1,0:T(8,128)(2,1)S(1)}, u32[]{:S(2)}, u32[]{:S(2)}) collective-permute-start(bf16[2064,128]{1,0:T(8,128)(2,1)S(1)} %fusion.1.refs_0_.own), channel_id=1, source_target_pairs={{0,2},{1,1023},{2,4},{3,1},{4,6},{5,3},{6,8},{7,5},{8,10},{9,7},{1... | collective-permute-start | bytes 1585160 | tf_op jit(solution)/shard_map/ppermute | solution.py:235
  10.5 9.3 %collective-permute-done.1.refs_2_ = bf16[2064,128]{1,0:T(8,128)(2,1)S(1)} collective-permute-done((bf16[2064,128]{1,0:T(8,128)(2,1)S(1)}, bf16[2064,128]{1,0:T(8,128)(2,1)S(1)}, u32[]{:S(2)}, u32[]{:S(2)}) %collective-permute-start.1) | collective-permute-done | bytes 528416 | tf_op jit(solution)/shard_map/ppermute | solution.py:235
  19.7 0.0 copy-start.1
  19.7 1.9 %collective-permute-start.5 = (bf16[2064,128]{1,0:T(8,128)(2,1)S(1)}, bf16[2064,128]{1,0:T(8,128)(2,1)S(1)}, u32[]{:S(2)}, u32[]{:S(2)}) collective-permute-start(bf16[2064,128]{1,0:T(8,128)(2,1)S(1)} %collective-permute-done.1.refs_2_), channel_id=1, source_target_pairs={{0,1022},{1,3},{2,0},{3,5},{4,2},{5,7},{6,4},{7,9},{8,6},{9,11},{1... | collective-permute-start | bytes 1585160 | tf_op jit(solution)/shard_map/ppermute | solution.py:235
  21.7 1.9 %collective-permute-start = (bf16[2064,128]{1,0:T(8,128)(2,1)S(1)}, bf16[2064,128]{1,0:T(8,128)(2,1)S(1)}, u32[]{:S(2)}, u32[]{:S(2)}) collective-permute-start(bf16[2064,128]{1,0:T(8,128)(2,1)S(1)} %fusion.1.refs_0_.own), channel_id=1, source_target_pairs={{0,1},{1,0},{2,3},{3,2},{4,5},{5,4},{6,7},{7,6},{8,9},{9,8},{10,11... | collective-permute-start | bytes 1585160 | tf_op jit(solution)/shard_map/ppermute | solution.py:235
  24.3 9.9 %psum.28 = s32[128]{0:T(128)S(1)} all-reduce(s32[128]{0:T(128)S(1)} %compare_select_fusion.2), channel_id=1, replica_groups=mesh['row'=32,'x'=4,'y'=4,'core'=2] {'x'}, use_global_device_ids=true, to_apply=%region_0.1 | all-reduce | flops 128 | bytes 1024 | tf_op jit(solution)/shard_map/psum | solution.py:250
  34.1 28.2 %psum.29 = s32[128]{0:T(128)S(1)} all-reduce(s32[128]{0:T(128)S(1)} %psum.28), channel_id=1, replica_groups=mesh['row'=32,'x'=4,'y'=4,'core'=2] {'y','core'}, use_global_device_ids=true, to_apply=%region_1.2 | all-reduce | flops 128 | bytes 1024 | tf_op jit(solution)/shard_map/psum | solution.py:251
  62.3 1.9 %collective-permute-start.2 = (bf16[2064,128]{1,0:T(8,128)(2,1)S(1)}, bf16[2064,128]{1,0:T(8,128)(2,1)S(1)}, u32[]{:S(2)}, u32[]{:S(2)}) collective-permute-start(bf16[2064,128]{1,0:T(8,128)(2,1)S(1)} %collective-permute-done.1.refs_2_), channel_id=1, source_target_pairs={{0,1},{1,0},{2,3},{3,2},{4,5},{5,4},{6,7},{7,6},{8,9},{9,8},{10,11... | collective-permute-start | bytes 1585160 | tf_op jit(solution)/shard_map/ppermute | solution.py:235
  64.2 0.7 fusion.2
  64.9 0.6 broadcast_in_dim.18
  65.6 1.9 %collective-permute-start.8 = (s32[128]{0:T(128)S(1)}, s32[128]{0:T(128)S(1)}, u32[]{:S(2)}, u32[]{:S(2)}) collective-permute-start(s32[128]{0:T(128)S(1)} %broadcast_in_dim.18), channel_id=1, source_target_pairs={{1,33},{2,66},{3,99},{4,132},{5,165},{6,198},{7,231},{8,264},{9,29... | collective-permute-start | bytes 1544 | tf_op jit(solution)/shard_map/ppermute | solution.py:235
  67.5 0.0 collective-permute-done.3.refs_0_
  67.5 0.0 copy-start.4
  67.5 1.9 %collective-permute-start.7 = (bf16[2064,128]{1,0:T(8,128)(2,1)S(1)}, bf16[2064,128]{1,0:T(8,128)(2,1)}, u32[]{:S(2)}, u32[]{:S(2)}) collective-permute-start(bf16[2064,128]{1,0:T(8,128)(2,1)S(1)} %collective-permute-done.3.refs_0_), channel_id=1, source_target_pairs={{0,2},{1,1023},{2,4},{3,1},{4,6},{5,3},{6,8},{7,5},{8,10},{9,7},{1... | collective-permute-start | bytes 1585160 | tf_op jit(solution)/shard_map/ppermute | solution.py:235
  69.5 8.5 %collective-permute-done.8 = s32[128]{0:T(128)S(1)} collective-permute-done((s32[128]{0:T(128)S(1)}, s32[128]{0:T(128)S(1)}, u32[]{:S(2)}, u32[]{:S(2)}) %collective-permute-start.8) | collective-permute-done | bytes 544 | tf_op jit(solution)/shard_map/ppermute | solution.py:235
  78.0 2.1 %collective-permute-start.4 = (bf16[2064,128]{1,0:T(8,128)(2,1)S(1)}, bf16[2064,128]{1,0:T(8,128)(2,1)}, u32[]{:S(2)}, u32[]{:S(2)}) collective-permute-start(bf16[2064,128]{1,0:T(8,128)(2,1)S(1)} %collective-permute-done.3.refs_0_), channel_id=1, source_target_pairs={{0,1},{1,0},{2,3},{3,2},{4,5},{5,4},{6,7},{7,6},{8,9},{9,8},{10,11... | collective-permute-start | bytes 1585160 | tf_op jit(solution)/shard_map/ppermute | solution.py:235
  80.1 0.0 collective-permute-done.5.refs_2_
  80.1 0.0 copy-start.5
  80.1 2.2 %collective-permute-start.6 = (bf16[2064,128]{1,0:T(8,128)(2,1)S(1)}, bf16[2064,128]{1,0:T(8,128)(2,1)}, u32[]{:S(2)}, u32[]{:S(2)}) collective-permute-start(bf16[2064,128]{1,0:T(8,128)(2,1)S(1)} %collective-permute-done.5.refs_2_), channel_id=1, source_target_pairs={{0,1},{1,0},{2,3},{3,2},{4,5},{5,4},{6,7},{7,6},{8,9},{9,8},{10,11... | collective-permute-start | bytes 1585160 | tf_op jit(solution)/shard_map/ppermute | solution.py:235
  82.3 0.1 reshape.29
  82.4 0.0 copy-done.6
  82.4 0.6 pad_add_fusion.params
  83.0 13.1 %psum.30 = s32[128]{0:T(128)S(1)} all-reduce(s32[128]{0:T(128)S(1)} %broadcast_select_fusion), channel_id=1, replica_groups=mesh['row'=32,'x'=4,'y'=4,'core'=2] {'x'}, use_global_device_ids=true, to_apply=%region_3.4 | all-reduce | flops 128 | bytes 1024 | tf_op jit(solution)/shard_map/psum | solution.py:256
  96.1 13.6 %psum.31 = s32[128]{0:T(128)S(1)} all-reduce(s32[128]{0:T(128)S(1)} %psum.30), channel_id=1, replica_groups=mesh['row'=32,'x'=4,'y'=4,'core'=2] {'y','core'}, use_global_device_ids=true, to_apply=%region_4.5 | all-reduce | flops 128 | bytes 1024 | tf_op jit(solution)/shard_map/psum | solution.py:257
  110.4 0.0 collective-permute-done.refs_1_
  110.4 0.0 copy-start.2
  110.4 0.0 collective-permute-done.2.refs_3_
  110.4 0.0 copy-done
  110.4 0.0 copy-done.1
  110.4 0.8 copy-done.2
  111.2 0.0 copy-start.3
  111.2 0.9 copy-done.3
  112.0 6.6 %early.1.acc_in = f32[66,128,128]{2,1,0:T(8,128)} custom-call(s32[84]{0:T(128)} %pad_add_fusion.params, bf16[2064,128]{1,0:T(8,128)(2,1)} %copy-done, bf16[2064,128]{1,0:T(8,128)(2,1)} %copy-done.2, bf16[2064,128]{1,0:T(8,128)(2,1)} %copy-done.1, bf16[2064,128]{1,0:T(8,128)(2,1)} %copy-done.3), custom_call_target="tpu_custom_call" | custom-call | flops 300000000 | bytes 4000000 | tf_op jit(solution)/shard_map/early/pallas_call | solution.py:169
  118.7 0.0 copy-done.4
  118.7 0.0 copy-done.5
  118.7 0.0 collective-permute-done.7.refs_4_
  118.7 0.0 collective-permute-done.4.refs_1_
  118.7 0.0 collective-permute-done.6.refs_3_
  118.7 8.7 %late.1 = bf16[66,128,128]{2,1,0:T(8,128)(2,1)} custom-call(s32[84]{0:T(128)} %pad_add_fusion.params, bf16[2064,128]{1,0:T(8,128)(2,1)} %copy-done, f32[66,128,128]{2,1,0:T(8,128)} %early.1.acc_in, bf16[2064,128]{1,0:T(8,128)(2,1)} %copy-done.4, bf16[2064,128]{1,0:T(8,128)(2,1)} %collective-permute-done.4.refs_1_, bf16[2064,128]{1,0:T(8,128)(2,1)} %copy-done.5, ...), custom_call_target="tpu_custom_call" | custom-call | flops 300000000 | bytes 6000000 | tf_op jit(solution)/shard_map/late/pallas_call | solution.py:193
  (3 shorter events, 0.0 us)
Async XLA Ops:
  0.6 81.8 %copy-start.6 = (s32[1,1,66]{2,1,0:T(1,128)S(1)}, s32[1,1,66]{2,1,0:T(1,128)}, u32[]{:S(2)}) copy-start(s32[1,1,66]{2,1,0:T(1,128)} %param.7) | copy-start | bytes 796
  2.5 107.9 %copy-start = (bf16[2064,128]{1,0:T(8,128)(2,1)}, bf16[2064,128]{1,0:T(8,128)(2,1)S(1)}, u32[]{:S(2)}) copy-start(bf16[2064,128]{1,0:T(8,128)(2,1)S(1)} %fusion.1.refs_0_.own) | copy-start | bytes 1585156
  2.5 17.2 %collective-permute-start.1 = (bf16[2064,128]{1,0:T(8,128)(2,1)S(1)}, bf16[2064,128]{1,0:T(8,128)(2,1)S(1)}, u32[]{:S(2)}, u32[]{:S(2)}) collective-permute-start(bf16[2064,128]{1,0:T(8,128)(2,1)S(1)} %fusion.1.refs_0_.own), channel_id=1, source_target_pairs={{0,1022},{1,3},{2,0},{3,5},{4,2},{5,7},{6,4},{7,9},{8,6},{9,11},{1... | collective-permute-start | bytes 1585160 | tf_op jit(solution)/shard_map/ppermute | solution.py:235
  5.2 62.3 %collective-permute-start.3 = (bf16[2064,128]{1,0:T(8,128)(2,1)S(1)}, bf16[2064,128]{1,0:T(8,128)(2,1)S(1)}, u32[]{:S(2)}, u32[]{:S(2)}) collective-permute-start(bf16[2064,128]{1,0:T(8,128)(2,1)S(1)} %fusion.1.refs_0_.own), channel_id=1, source_target_pairs={{0,2},{1,1023},{2,4},{3,1},{4,6},{5,3},{6,8},{7,5},{8,10},{9,7},{1... | collective-permute-start | bytes 1585160 | tf_op jit(solution)/shard_map/ppermute | solution.py:235
  19.7 90.7 %copy-start.1 = (bf16[2064,128]{1,0:T(8,128)(2,1)}, bf16[2064,128]{1,0:T(8,128)(2,1)S(1)}, u32[]{:S(2)}) copy-start(bf16[2064,128]{1,0:T(8,128)(2,1)S(1)} %collective-permute-done.1.refs_2_) | copy-start | bytes 1585156
  19.7 60.4 %collective-permute-start.5 = (bf16[2064,128]{1,0:T(8,128)(2,1)S(1)}, bf16[2064,128]{1,0:T(8,128)(2,1)S(1)}, u32[]{:S(2)}, u32[]{:S(2)}) collective-permute-start(bf16[2064,128]{1,0:T(8,128)(2,1)S(1)} %collective-permute-done.1.refs_2_), channel_id=1, source_target_pairs={{0,1022},{1,3},{2,0},{3,5},{4,2},{5,7},{6,4},{7,9},{8,6},{9,11},{1... | collective-permute-start | bytes 1585160 | tf_op jit(solution)/shard_map/ppermute | solution.py:235
  21.7 88.7 %collective-permute-start = (bf16[2064,128]{1,0:T(8,128)(2,1)S(1)}, bf16[2064,128]{1,0:T(8,128)(2,1)S(1)}, u32[]{:S(2)}, u32[]{:S(2)}) collective-permute-start(bf16[2064,128]{1,0:T(8,128)(2,1)S(1)} %fusion.1.refs_0_.own), channel_id=1, source_target_pairs={{0,1},{1,0},{2,3},{3,2},{4,5},{5,4},{6,7},{7,6},{8,9},{9,8},{10,11... | collective-permute-start | bytes 1585160 | tf_op jit(solution)/shard_map/ppermute | solution.py:235
  62.3 48.1 %collective-permute-start.2 = (bf16[2064,128]{1,0:T(8,128)(2,1)S(1)}, bf16[2064,128]{1,0:T(8,128)(2,1)S(1)}, u32[]{:S(2)}, u32[]{:S(2)}) collective-permute-start(bf16[2064,128]{1,0:T(8,128)(2,1)S(1)} %collective-permute-done.1.refs_2_), channel_id=1, source_target_pairs={{0,1},{1,0},{2,3},{3,2},{4,5},{5,4},{6,7},{7,6},{8,9},{9,8},{10,11... | collective-permute-start | bytes 1585160 | tf_op jit(solution)/shard_map/ppermute | solution.py:235
  65.6 12.4 %collective-permute-start.8 = (s32[128]{0:T(128)S(1)}, s32[128]{0:T(128)S(1)}, u32[]{:S(2)}, u32[]{:S(2)}) collective-permute-start(s32[128]{0:T(128)S(1)} %broadcast_in_dim.18), channel_id=1, source_target_pairs={{1,33},{2,66},{3,99},{4,132},{5,165},{6,198},{7,231},{8,264},{9,29... | collective-permute-start | bytes 1544 | tf_op jit(solution)/shard_map/ppermute | solution.py:235
  67.5 51.1 %copy-start.4 = (bf16[2064,128]{1,0:T(8,128)(2,1)}, bf16[2064,128]{1,0:T(8,128)(2,1)S(1)}, u32[]{:S(2)}) copy-start(bf16[2064,128]{1,0:T(8,128)(2,1)S(1)} %collective-permute-done.3.refs_0_) | copy-start | bytes 1585156
  67.5 51.1 %collective-permute-start.7 = (bf16[2064,128]{1,0:T(8,128)(2,1)S(1)}, bf16[2064,128]{1,0:T(8,128)(2,1)}, u32[]{:S(2)}, u32[]{:S(2)}) collective-permute-start(bf16[2064,128]{1,0:T(8,128)(2,1)S(1)} %collective-permute-done.3.refs_0_), channel_id=1, source_target_pairs={{0,2},{1,1023},{2,4},{3,1},{4,6},{5,3},{6,8},{7,5},{8,10},{9,7},{1... | collective-permute-start | bytes 1585160 | tf_op jit(solution)/shard_map/ppermute | solution.py:235
  78.0 40.7 %collective-permute-start.4 = (bf16[2064,128]{1,0:T(8,128)(2,1)S(1)}, bf16[2064,128]{1,0:T(8,128)(2,1)}, u32[]{:S(2)}, u32[]{:S(2)}) collective-permute-start(bf16[2064,128]{1,0:T(8,128)(2,1)S(1)} %collective-permute-done.3.refs_0_), channel_id=1, source_target_pairs={{0,1},{1,0},{2,3},{3,2},{4,5},{5,4},{6,7},{7,6},{8,9},{9,8},{10,11... | collective-permute-start | bytes 1585160 | tf_op jit(solution)/shard_map/ppermute | solution.py:235
  80.1 38.5 %copy-start.5 = (bf16[2064,128]{1,0:T(8,128)(2,1)}, bf16[2064,128]{1,0:T(8,128)(2,1)S(1)}, u32[]{:S(2)}) copy-start(bf16[2064,128]{1,0:T(8,128)(2,1)S(1)} %collective-permute-done.5.refs_2_) | copy-start | bytes 1585156
  80.1 38.6 %collective-permute-start.6 = (bf16[2064,128]{1,0:T(8,128)(2,1)S(1)}, bf16[2064,128]{1,0:T(8,128)(2,1)}, u32[]{:S(2)}, u32[]{:S(2)}) collective-permute-start(bf16[2064,128]{1,0:T(8,128)(2,1)S(1)} %collective-permute-done.5.refs_2_), channel_id=1, source_target_pairs={{0,1},{1,0},{2,3},{3,2},{4,5},{5,4},{6,7},{7,6},{8,9},{9,8},{10,11... | collective-permute-start | bytes 1585160 | tf_op jit(solution)/shard_map/ppermute | solution.py:235
  110.4 0.8 copy-start.2
  111.2 0.9 copy-start.3

commit v3 on v1

v3 whole, which is shorter than its diff:
```python
import functools

import jax
import jax.numpy as jnp
from jax import lax
from jax.experimental import pallas as pl
from jax.experimental.pallas import tpu as pltpu
from jax.sharding import Mesh, PartitionSpec as P


H = 8
LANES = 128
COPIES = 4
META_ROWS = 16
ALL = ("row", "x", "y", "core")

OWN, I0, S1, S2, I1, I2, F1, I3, F2 = range(9)
SIDE_STEPS = {OWN: 0, I0: 1, S1: 2, S2: -2, I1: -1, I2: 3, F1: 4, I3: -3, F2: -4}


def chip_pairs(devices, step):
    return [(d, (d + 2 * (step if d % 2 == 0 else -step)) % devices) for d in range(devices)]


def core_pairs(devices):
    return [(d, d ^ 1) for d in range(devices)]


def product_kernel(slots, params, *refs):
    pieces = refs[:9]
    out, near, acc, meta_raw, meta_vec, stage, meta, load_sems, meta_sems, meta_sem, out_sems = refs[9:]
    tiles, size = acc.shape[:2]
    band = tiles // 2
    rows = 2 * slots * size
    reach = 2 * H + 2
    side = params[0]
    count = params[1]
    metas = []
    loads = []
    for p in range(9):
        copy = pltpu.make_async_copy(pieces[p].at[pl.ds(rows, META_ROWS)], meta_raw.at[p], meta_sems.at[p])
        copy.start()
        metas.append(copy)
    for p in range(9):
        copy = pltpu.make_async_copy(pieces[p].at[pl.ds(0, rows)], near.at[p], load_sems.at[p])
        copy.start()
        loads.append(copy)
    for p in range(9):
        metas[p].wait()
        meta_vec[2 * p:2 * p + 2, :] = meta_raw[p].astype(jnp.float32)[0:2, :].astype(jnp.int32)
    to_smem = pltpu.make_async_copy(meta_vec, meta, meta_sem)
    to_smem.start()
    acc[...] = jnp.zeros_like(acc)
    to_smem.wait()
    for p in range(9):
        loads[p].wait()
        base = 2 * (SIDE_STEPS[p] * side + H // 2)

        @pl.loop(0, 4)
        def _(j):
            b = j // 2
            a = j - 2 * b
            rel = base + b
            t = params[2 + a * reach + rel]

            @pl.when(t >= 0)
            def _():
                a_block = near[OWN, pl.ds(pl.multiple_of((a * slots + t) * size, size), size), :]
                shift = a * band + rel + H - a
                for u in range(0, slots, 2):
                    start = pl.multiple_of((b * slots + u) * size, size)
                    pair = jnp.concatenate(
                        [near[p, pl.ds(start, size), :], near[p, pl.ds(start + size, size), :]], axis=1
                    )
                    both = jnp.dot(a_block, pair, preferred_element_type=jnp.float32)
                    f = shift + meta[2 * p + b, u]
                    acc[f] = acc[f] + both[:, :size]
                    g = shift + meta[2 * p + b, u + 1]
                    acc[g] = acc[g] + both[:, size:]

    chunks = out_sems.shape[0]
    per = tiles // chunks
    stores = []
    for c in range(chunks):

        @pl.loop(c * per, (c + 1) * per)
        def _(p):
            @pl.when(p < count)
            def _():
                stage[p] = acc[params[2 + 2 * reach + p]].astype(stage.dtype)

            @pl.when(p >= count)
            def _():
                stage[p] = jnp.zeros((size, size), stage.dtype)

        copy = pltpu.make_async_copy(stage.at[pl.ds(c * per, per)], out.at[pl.ds(c * per, per)], out_sems.at[c])
        copy.start()
        stores.append(copy)
    for copy in stores:
        copy.wait()


def products(params, pieces, tiles, size, slots):
    chunks = 6
    return pl.pallas_call(
        functools.partial(product_kernel, slots),
        out_shape=jax.ShapeDtypeStruct((tiles, size, size), jnp.bfloat16),
        in_specs=[pl.BlockSpec(memory_space=pltpu.SMEM)] + [pl.BlockSpec(memory_space=pl.ANY)] * 9,
        out_specs=pl.BlockSpec(memory_space=pl.ANY),
        scratch_shapes=[
            pltpu.VMEM((9, 2 * slots * size, LANES), jnp.bfloat16),
            pltpu.VMEM((tiles, size, size), jnp.float32),
            pltpu.VMEM((9, META_ROWS, LANES), jnp.bfloat16),
            pltpu.VMEM((24, LANES), jnp.int32),
            pltpu.VMEM((tiles, size, size), jnp.bfloat16),
            pltpu.SMEM((24, LANES), jnp.int32),
            pltpu.SemaphoreType.DMA((9,)),
            pltpu.SemaphoreType.DMA((9,)),
            pltpu.SemaphoreType.DMA,
            pltpu.SemaphoreType.DMA((chunks,)),
        ],
        compiler_params=pltpu.CompilerParams(vmem_limit_bytes=24 * 1024 * 1024),
        cost_estimate=pl.CostEstimate(flops=600_000_000, bytes_accessed=8_000_000, transcendentals=0),
        name="products",
    )(params, *pieces)


def make_shards(shape):
    rows_of = shape["row"]
    cols_of = shape["x"] * shape["y"] * shape["core"]
    devices = rows_of * cols_of

    def compute(blocks, colidx, counts, out_list):
        here, slots, size = blocks.shape[:3]
        grid_row = lax.axis_index("row")
        col = lax.axis_index(("x", "y", "core"))
        device = grid_row * cols_of + col
        total = here * devices
        row_ids = device * here + jnp.arange(here, dtype=jnp.int32)[:, None]
        away = colidx - row_ids
        away = jnp.where(away > H, away - total, jnp.where(away < -H, away + total, away))
        meta = jnp.pad(away.astype(jnp.bfloat16), ((0, META_ROWS - here), (0, LANES - slots)))
        own = jnp.concatenate([blocks.reshape(here * slots * size, size), meta], axis=0)

        def send(x, pairs):
            return lax.ppermute(x, ALL, pairs)

        down, up, swap = chip_pairs(devices, -1), chip_pairs(devices, 1), core_pairs(devices)
        s1 = send(own, down)
        s2 = send(own, up)
        f1 = send(s1, down)
        f2 = send(s2, up)
        i0 = send(own, swap)
        i1 = send(s1, swap)
        i2 = send(s2, swap)
        i3 = send(f1, swap)

        mine = lax.optimization_barrier(jnp.broadcast_to(counts, (COPIES, LANES)))
        all_counts = lax.optimization_barrier(lax.all_gather(mine, ALL, axis=0, tiled=True))
        first = all_counts.reshape(devices, COPIES, LANES)[:, 0, :]
        earlier = jnp.arange(devices, dtype=jnp.int32)[:, None] < device
        offsets = jnp.sum(jnp.where(earlier, first, 0), axis=0)[:1].astype(jnp.int32).reshape(1, 1)

        side = 1 - 2 * (col % 2)
        tiles = here * (4 * H + 1)
        reach = jnp.arange(2 * H + 2, dtype=jnp.int32)
        spot = away + H + jnp.arange(here, dtype=jnp.int32)[:, None]
        hit = spot[:, :, None] == reach[None, None, :]
        slot = jnp.sum(jnp.where(hit, jnp.arange(1, slots + 1, dtype=jnp.int32)[None, :, None], 0), axis=1) - 1
        params = jnp.concatenate(
            [side.reshape(1), counts.reshape(1), slot.reshape(-1), out_list.reshape(-1)]
        ).astype(jnp.int32)
        by_name = {OWN: own, I0: i0, S1: s1, S2: s2, I1: i1, I2: i2, F1: f1, I3: i3, F2: f2}
        packed = products(params, [by_name[p] for p in range(9)], tiles, size, slots)
        return (packed, offsets)

    return compute


def solution(mesh):
    rows_of, cols_of = mesh.shape["row"], mesh.shape["col"]
    fine = Mesh(mesh.devices.reshape(rows_of, cols_of // 8, 4, 2), ALL)
    col = ("x", "y", "core")
    in_specs = (
        P(ALL, None, None, None),
        P(ALL, None),
        P("row", col),
        P("row", col, None),
    )
    out_specs = (P(ALL, None, None), P("row", col))
    return jax.shard_map(
        make_shards(dict(fine.shape)), mesh=fine, in_specs=in_specs, out_specs=out_specs, check_vma=False
    )
```

time: 118 us -> 355 us (3.01)
  the two profiles are of different devices: /device:TPU:24 before, /device:TPU:1 now
where the time goes in v3:
time: 355 us; the launch traced here: 354 us
  waiting for transfers between devices  273 us (77%)
  starting transfers between devices  52.1 us (15%)
  between operations  14.8 us (4%)
  Pallas kernels  9 us (3%)
    all_gather x1, waiting for transfers between devices, compute(): lax.all_gather(mine, ALL, axis=0, tiled=True)  267 us
    ppermute x8, starting transfers between devices, send(): return lax.ppermute(x, ALL, pairs)  52 us
    pallas_call x1, Pallas kernels, products(): pl.pallas_call(functools.partial(product_kernel, slots), out_shape=jax.Sh...  9 us
  transfers between devices with their start and end apart: 9, of which 4 were waited for; matrix products, arithmetic and copies ran while one was open for 1% of the time, Pallas kernels for 3%

profile of v3, /device:TPU:1, one launch (start us, length us, event | category | flops | bytes accessed | tf_op | source)
XLA Modules:
  0.0 354.1 jit_solution(13552314072542829213)
XLA Ops:
  7.2 0.0 copy-start
  7.2 0.0 all-gather.3.cloned.1.call-start
  7.9 0.6 broadcast_in_dim.41
  8.5 0.0 all-gather.3.cloned.1.call-update
  8.5 0.8 fusion.2
  9.3 1.1 fusion.1.refs_0_
  10.3 4.0 %collective-permute-start.1 = (bf16[2064,128]{1,0:T(8,128)(2,1)S(1)}, bf16[2064,128]{1,0:T(8,128)(2,1)S(1)}, u32[]{:S(2)}, u32[]{:S(2)}) collective-permute-start(bf16[2064,128]{1,0:T(8,128)(2,1)S(1)} %fusion.1.refs_0_), channel_id=1, source_target_pairs={{0,1022},{1,3},{2,0},{3,5},{4,2},{5,7},{6,4},{7,9},{8,6},{9,11},{1... | collective-permute-start | bytes 1585160 | tf_op jit(solution)/shard_map/ppermute | solution.py:146
  14.4 21.8 %collective-permute-start.2 = (bf16[2064,128]{1,0:T(8,128)(2,1)S(1)}, bf16[2064,128]{1,0:T(8,128)(2,1)S(1)}, u32[]{:S(2)}, u32[]{:S(2)}) collective-permute-start(bf16[2064,128]{1,0:T(8,128)(2,1)S(1)} %fusion.1.refs_0_), channel_id=1, source_target_pairs={{0,2},{1,1023},{2,4},{3,1},{4,6},{5,3},{6,8},{7,5},{8,10},{9,7},{1... | collective-permute-start | bytes 1585160 | tf_op jit(solution)/shard_map/ppermute | solution.py:146
  36.1 4.7 %collective-permute-done.1.refs_2_ = bf16[2064,128]{1,0:T(8,128)(2,1)S(1)} collective-permute-done((bf16[2064,128]{1,0:T(8,128)(2,1)S(1)}, bf16[2064,128]{1,0:T(8,128)(2,1)S(1)}, u32[]{:S(2)}, u32[]{:S(2)}) %collective-permute-start.1) | collective-permute-done | bytes 528416 | tf_op jit(solution)/shard_map/ppermute | solution.py:146
  40.8 1.9 collective-permute-start.5
  42.7 15.8 %collective-permute-start = (bf16[2064,128]{1,0:T(8,128)(2,1)S(1)}, bf16[2064,128]{1,0:T(8,128)(2,1)S(1)}, u32[]{:S(2)}, u32[]{:S(2)}) collective-permute-start(bf16[2064,128]{1,0:T(8,128)(2,1)S(1)} %fusion.1.refs_0_), channel_id=1, source_target_pairs={{0,1},{1,0},{2,3},{3,2},{4,5},{5,4},{6,7},{7,6},{8,9},{9,8},{10,11... | collective-permute-start | bytes 1585160 | tf_op jit(solution)/shard_map/ppermute | solution.py:146
  58.5 0.0 collective-permute-done.2.refs_3_
  58.5 1.9 collective-permute-start.7
  60.5 1.9 collective-permute-start.4
  62.4 2.4 collective-permute-start.3
  64.8 0.0 collective-permute-done.5.refs_6_
  64.8 2.3 collective-permute-start.6
  67.1 0.1 select_reduce_fusion.1
  67.2 0.1 sub.25
  67.3 0.0 copy-done
  67.3 0.1 pad_add_fusion.params
  67.4 0.0 collective-permute-done.refs_1_
  67.4 1.1 collective-permute-done.7.refs_8_
  68.6 0.0 collective-permute-done.4.refs_5_
  68.6 0.0 collective-permute-done.3.refs_4_
  68.6 0.2 collective-permute-done.6.refs_7_
  68.8 9.0 %products.1 = bf16[66,128,128]{2,1,0:T(8,128)(2,1)} custom-call(s32[104]{0:T(128)S(1)} %pad_add_fusion.params, bf16[2064,128]{1,0:T(8,128)(2,1)S(1)} %fusion.1.refs_0_, bf16[2064,128]{1,0:T(8,128)(2,1)S(1)} %collective-permute-done.refs_1_, bf16[2064,128]{1,0:T(8,128)(2,1)S(1)} %collective-permute-done.1.refs_2_, ...), custom_call_target="tpu_custom_call" | custom-call | flops 600000000 | bytes 8000000 | tf_op jit(solution)/shard_map/products/pallas_call | solution.py:105
  77.8 266.8 %all-gather.3.cloned.1.call-done = s32[1024,4,128]{2,1,0:T(4,128)} async-done(((s32[1,4,128]{2,1,0:T(4,128)}), s32[1024,4,128]{2,1,0:T(4,128)}) %all-gather.3.cloned.1.call-update) | async-done | bytes 2097168 | tf_op jit(solution)/shard_map/all_gather | solution.py:159
  344.6 2.0 slice.8
  346.6 0.7 select_reduce_fusion
  (5 shorter events, 0.0 us)
Async XLA Ops:
  7.2 60.2 %copy-start = (s32[1,1,66]{2,1,0:T(1,128)S(1)}, s32[1,1,66]{2,1,0:T(1,128)}, u32[]{:S(2)}) copy-start(s32[1,1,66]{2,1,0:T(1,128)} %param.7) | copy-start | bytes 796
  7.2 337.4 %all-gather.3.cloned.1.call-start = ((), (), s32[]{:S(2)}) async-start(), calls=%async_computation | async-start | bytes 2099200 | tf_op jit(solution)/shard_map/all_gather | solution.py:159
  10.3 30.5 %collective-permute-start.1 = (bf16[2064,128]{1,0:T(8,128)(2,1)S(1)}, bf16[2064,128]{1,0:T(8,128)(2,1)S(1)}, u32[]{:S(2)}, u32[]{:S(2)}) collective-permute-start(bf16[2064,128]{1,0:T(8,128)(2,1)S(1)} %fusion.1.refs_0_), channel_id=1, source_target_pairs={{0,1022},{1,3},{2,0},{3,5},{4,2},{5,7},{6,4},{7,9},{8,6},{9,11},{1... | collective-permute-start | bytes 1585160 | tf_op jit(solution)/shard_map/ppermute | solution.py:146
  14.4 44.1 %collective-permute-start.2 = (bf16[2064,128]{1,0:T(8,128)(2,1)S(1)}, bf16[2064,128]{1,0:T(8,128)(2,1)S(1)}, u32[]{:S(2)}, u32[]{:S(2)}) collective-permute-start(bf16[2064,128]{1,0:T(8,128)(2,1)S(1)} %fusion.1.refs_0_), channel_id=1, source_target_pairs={{0,2},{1,1023},{2,4},{3,1},{4,6},{5,3},{6,8},{7,5},{8,10},{9,7},{1... | collective-permute-start | bytes 1585160 | tf_op jit(solution)/shard_map/ppermute | solution.py:146
  40.8 24.0 %collective-permute-start.5 = (bf16[2064,128]{1,0:T(8,128)(2,1)S(1)}, bf16[2064,128]{1,0:T(8,128)(2,1)S(1)}, u32[]{:S(2)}, u32[]{:S(2)}) collective-permute-start(bf16[2064,128]{1,0:T(8,128)(2,1)S(1)} %collective-permute-done.1.refs_2_), channel_id=1, source_target_pairs={{0,1022},{1,3},{2,0},{3,5},{4,2},{5,7},{6,4},{7,9},{8,6},{9,11},{1... | collective-permute-start | bytes 1585160 | tf_op jit(solution)/shard_map/ppermute | solution.py:146
  42.7 24.7 %collective-permute-start = (bf16[2064,128]{1,0:T(8,128)(2,1)S(1)}, bf16[2064,128]{1,0:T(8,128)(2,1)S(1)}, u32[]{:S(2)}, u32[]{:S(2)}) collective-permute-start(bf16[2064,128]{1,0:T(8,128)(2,1)S(1)} %fusion.1.refs_0_), channel_id=1, source_target_pairs={{0,1},{1,0},{2,3},{3,2},{4,5},{5,4},{6,7},{7,6},{8,9},{9,8},{10,11... | collective-permute-start | bytes 1585160 | tf_op jit(solution)/shard_map/ppermute | solution.py:146
  58.5 10.0 %collective-permute-start.7 = (bf16[2064,128]{1,0:T(8,128)(2,1)S(1)}, bf16[2064,128]{1,0:T(8,128)(2,1)S(1)}, u32[]{:S(2)}, u32[]{:S(2)}) collective-permute-start(bf16[2064,128]{1,0:T(8,128)(2,1)S(1)} %collective-permute-done.2.refs_3_), channel_id=1, source_target_pairs={{0,2},{1,1023},{2,4},{3,1},{4,6},{5,3},{6,8},{7,5},{8,10},{9,7},{1... | collective-permute-start | bytes 1585160 | tf_op jit(solution)/shard_map/ppermute | solution.py:146
  60.5 8.1 %collective-permute-start.4 = (bf16[2064,128]{1,0:T(8,128)(2,1)S(1)}, bf16[2064,128]{1,0:T(8,128)(2,1)}, u32[]{:S(2)}, u32[]{:S(2)}) collective-permute-start(bf16[2064,128]{1,0:T(8,128)(2,1)S(1)} %collective-permute-done.2.refs_3_), channel_id=1, source_target_pairs={{0,1},{1,0},{2,3},{3,2},{4,5},{5,4},{6,7},{7,6},{8,9},{9,8},{10,11... | collective-permute-start | bytes 1585160 | tf_op jit(solution)/shard_map/ppermute | solution.py:146
  62.4 6.2 %collective-permute-start.3 = (bf16[2064,128]{1,0:T(8,128)(2,1)S(1)}, bf16[2064,128]{1,0:T(8,128)(2,1)}, u32[]{:S(2)}, u32[]{:S(2)}) collective-permute-start(bf16[2064,128]{1,0:T(8,128)(2,1)S(1)} %collective-permute-done.1.refs_2_), channel_id=1, source_target_pairs={{0,1},{1,0},{2,3},{3,2},{4,5},{5,4},{6,7},{7,6},{8,9},{9,8},{10,11... | collective-permute-start | bytes 1585160 | tf_op jit(solution)/shard_map/ppermute | solution.py:146
  64.8 4.0 %collective-permute-start.6 = (bf16[2064,128]{1,0:T(8,128)(2,1)S(1)}, bf16[2064,128]{1,0:T(8,128)(2,1)}, u32[]{:S(2)}, u32[]{:S(2)}) collective-permute-start(bf16[2064,128]{1,0:T(8,128)(2,1)S(1)} %collective-permute-done.5.refs_6_), channel_id=1, source_target_pairs={{0,1},{1,0},{2,3},{3,2},{4,5},{5,4},{6,7},{7,6},{8,9},{9,8},{10,11... | collective-permute-start | bytes 1585160 | tf_op jit(solution)/shard_map/ppermute | solution.py:146
Sparse Core Ops, SparseCore 0:
  13.8 330.7 all-gather.2

commit v4 on v3

--- a/solution.py
+++ b/solution.py
@@ -10,7 +10,6 @@
 
 H = 8
 LANES = 128
-COPIES = 4
 META_ROWS = 16
 ALL = ("row", "x", "y", "core")
 
@@ -24,6 +23,10 @@
 
 def core_pairs(devices):
     return [(d, d ^ 1) for d in range(devices)]
+
+
+def far_pairs(rows, cols):
+    return [(r * cols + c, (r + c) % rows * cols + c) for r in range(rows) for c in range(1, cols)]
 
 
 def product_kernel(slots, params, *refs):
@@ -45,12 +48,12 @@
         copy = pltpu.make_async_copy(pieces[p].at[pl.ds(0, rows)], near.at[p], load_sems.at[p])
         copy.start()
         loads.append(copy)
+    acc[...] = jnp.zeros_like(acc)
     for p in range(9):
         metas[p].wait()
         meta_vec[2 * p:2 * p + 2, :] = meta_raw[p].astype(jnp.float32)[0:2, :].astype(jnp.int32)
     to_smem = pltpu.make_async_copy(meta_vec, meta, meta_sem)
     to_smem.start()
-    acc[...] = jnp.zeros_like(acc)
     to_smem.wait()
     for p in range(9):
         loads[p].wait()
@@ -155,11 +158,17 @@
         i2 = send(s2, swap)
         i3 = send(f1, swap)
 
-        mine = lax.optimization_barrier(jnp.broadcast_to(counts, (COPIES, LANES)))
-        all_counts = lax.optimization_barrier(lax.all_gather(mine, ALL, axis=0, tiled=True))
-        first = all_counts.reshape(devices, COPIES, LANES)[:, 0, :]
-        earlier = jnp.arange(devices, dtype=jnp.int32)[:, None] < device
-        offsets = jnp.sum(jnp.where(earlier, first, 0), axis=0)[:1].astype(jnp.int32).reshape(1, 1)
+        lane = jnp.arange(LANES, dtype=jnp.int32)
+        row_counts = jnp.where(lane == col, counts[0, 0], 0)
+        row_counts = lax.psum(row_counts, ("y", "core"))
+        row_counts = lax.psum(row_counts, "x")
+        within = jnp.sum(jnp.where(lane < col, row_counts, 0))
+        row_total = jnp.broadcast_to(jnp.sum(row_counts), (LANES,))
+        far = send(row_total, far_pairs(rows_of, cols_of))
+        before = jnp.where((col >= 1) & (col <= grid_row), far, 0)
+        before = lax.psum(before, ("y", "core"))
+        before = lax.psum(before, "x")
+        offsets = (before[0] + within).astype(jnp.int32).reshape(1, 1)
 
         side = 1 - 2 * (col % 2)
         tiles = here * (4 * H + 1)

time: 355 us -> 104 us (0.29)
  the two profiles are of different devices: /device:TPU:1 before, /device:TPU:24 now
where the time goes in v4:
time: 104 us; the launch traced here: 103 us
  blocking collectives  59.4 us (57%)
  starting transfers between devices  26 us (25%)
  Pallas kernels  8.71 us (8%)
  between operations  3.29 us (3%)
  other arithmetic  2.72 us (3%)
  waiting for transfers between devices  2.39 us (2%)
    ppermute x9, starting transfers between devices, send(): return lax.ppermute(x, ALL, pairs)  26 us
    psum x1, blocking collectives, compute(): row_counts = lax.psum(row_counts, ('y', 'core'))  25.3 us
    psum x1, blocking collectives, compute(): before = lax.psum(before, 'x')  19.1 us
    psum x1, blocking collectives, compute(): before = lax.psum(before, ('y', 'core'))  9.22 us
    pallas_call x1, Pallas kernels, products(): pl.pallas_call(functools.partial(product_kernel, slots), out_shape=jax.Sh...  8.71 us
    psum x1, blocking collectives, compute(): row_counts = lax.psum(row_counts, 'x')  5.76 us
    ppermute x9, waiting for transfers between devices, send(): return lax.ppermute(x, ALL, pairs)  2.39 us
  transfers between devices with their start and end apart: 9, of which 1 were waited for; matrix products, arithmetic and copies ran while one was open for 2% of the time, Pallas kernels for 0%

profile of v4, /device:TPU:24, one launch (start us, length us, event | category | flops | bytes accessed | tf_op | source)
XLA Modules:
  0.0 103.2 jit_solution(14765403147662026511)
XLA Ops:
  0.6 0.0 copy-start
  0.7 0.8 fusion.3
  1.4 1.1 %fusion.1.refs_0_ = bf16[2064,128]{1,0:T(8,128)(2,1)S(1)} fusion(bf16[2,8]{1,0:T(2,128)(2,1)S(1)} %get-tuple-element.4, bf16[2048,128]{1,0:T(8,128)(2,1)} %bitcast.10), kind=kLoop, calls=%fused_computation.2 | loop fusion | flops 1585152 | bytes 1052704 | tf_op jit(solution)/shard_map/concatenate | solution.py:146
  2.5 2.7 %collective-permute-start.1 = (bf16[2064,128]{1,0:T(8,128)(2,1)S(1)}, bf16[2064,128]{1,0:T(8,128)(2,1)S(1)}, u32[]{:S(2)}, u32[]{:S(2)}) collective-permute-start(bf16[2064,128]{1,0:T(8,128)(2,1)S(1)} %fusion.1.refs_0_), channel_id=1, source_target_pairs={{0,1022},{1,3},{2,0},{3,5},{4,2},{5,7},{6,4},{7,9},{8,6},{9,11},{1... | collective-permute-start | bytes 1585160 | tf_op jit(solution)/shard_map/ppermute | solution.py:149
  5.2 5.3 %collective-permute-start.2 = (bf16[2064,128]{1,0:T(8,128)(2,1)S(1)}, bf16[2064,128]{1,0:T(8,128)(2,1)S(1)}, u32[]{:S(2)}, u32[]{:S(2)}) collective-permute-start(bf16[2064,128]{1,0:T(8,128)(2,1)S(1)} %fusion.1.refs_0_), channel_id=1, source_target_pairs={{0,2},{1,1023},{2,4},{3,1},{4,6},{5,3},{6,8},{7,5},{8,10},{9,7},{1... | collective-permute-start | bytes 1585160 | tf_op jit(solution)/shard_map/ppermute | solution.py:149
  10.5 1.9 %collective-permute-start = (bf16[2064,128]{1,0:T(8,128)(2,1)S(1)}, bf16[2064,128]{1,0:T(8,128)(2,1)S(1)}, u32[]{:S(2)}, u32[]{:S(2)}) collective-permute-start(bf16[2064,128]{1,0:T(8,128)(2,1)S(1)} %fusion.1.refs_0_), channel_id=1, source_target_pairs={{0,1},{1,0},{2,3},{3,2},{4,5},{5,4},{6,7},{7,6},{8,9},{9,8},{10,11... | collective-permute-start | bytes 1585160 | tf_op jit(solution)/shard_map/ppermute | solution.py:149
  13.1 25.3 %psum.28 = s32[128]{0:T(128)S(1)} all-reduce(s32[128]{0:T(128)S(1)} %compare_select_fusion.2), channel_id=1, replica_groups=mesh['row'=32,'x'=4,'y'=4,'core'=2] {'y','core'}, use_global_device_ids=true, to_apply=%region_1.2 | all-reduce | flops 128 | bytes 1024 | tf_op jit(solution)/shard_map/psum | solution.py:163
  38.4 5.8 %psum.29 = s32[128]{0:T(128)S(1)} all-reduce(s32[128]{0:T(128)S(1)} %psum.28), channel_id=1, replica_groups=mesh['row'=32,'x'=4,'y'=4,'core'=2] {'x'}, use_global_device_ids=true, to_apply=%region_2.3 | all-reduce | flops 128 | bytes 1024 | tf_op jit(solution)/shard_map/psum | solution.py:164
  44.1 0.0 collective-permute-done.1.refs_2_
  44.1 1.9 %collective-permute-start.5 = (bf16[2064,128]{1,0:T(8,128)(2,1)S(1)}, bf16[2064,128]{1,0:T(8,128)(2,1)S(1)}, u32[]{:S(2)}, u32[]{:S(2)}) collective-permute-start(bf16[2064,128]{1,0:T(8,128)(2,1)S(1)} %collective-permute-done.1.refs_2_), channel_id=1, source_target_pairs={{0,1022},{1,3},{2,0},{3,5},{4,2},{5,7},{6,4},{7,9},{8,6},{9,11},{1... | collective-permute-start | bytes 1585160 | tf_op jit(solution)/shard_map/ppermute | solution.py:149
  46.0 0.7 fusion.2
  46.7 0.6 broadcast_in_dim.36
  47.4 1.9 %collective-permute-start.8 = (s32[128]{0:T(128)S(1)}, s32[128]{0:T(128)S(1)}, u32[]{:S(2)}, u32[]{:S(2)}) collective-permute-start(s32[128]{0:T(128)S(1)} %broadcast_in_dim.36), channel_id=1, source_target_pairs={{1,33},{2,66},{3,99},{4,132},{5,165},{6,198},{7,231},{8,264},{9,29... | collective-permute-start | bytes 1544 | tf_op jit(solution)/shard_map/ppermute | solution.py:149
  49.3 0.1 select_reduce_fusion
  49.4 0.0 collective-permute-done.2.refs_3_
  49.4 6.0 %collective-permute-start.7 = (bf16[2064,128]{1,0:T(8,128)(2,1)S(1)}, bf16[2064,128]{1,0:T(8,128)(2,1)S(1)}, u32[]{:S(2)}, u32[]{:S(2)}) collective-permute-start(bf16[2064,128]{1,0:T(8,128)(2,1)S(1)} %collective-permute-done.2.refs_3_), channel_id=1, source_target_pairs={{0,2},{1,1023},{2,4},{3,1},{4,6},{5,3},{6,8},{7,5},{8,10},{9,7},{1... | collective-permute-start | bytes 1585160 | tf_op jit(solution)/shard_map/ppermute | solution.py:149
  55.5 1.9 %collective-permute-start.4 = (bf16[2064,128]{1,0:T(8,128)(2,1)S(1)}, bf16[2064,128]{1,0:T(8,128)(2,1)}, u32[]{:S(2)}, u32[]{:S(2)}) collective-permute-start(bf16[2064,128]{1,0:T(8,128)(2,1)S(1)} %collective-permute-done.2.refs_3_), channel_id=1, source_target_pairs={{0,1},{1,0},{2,3},{3,2},{4,5},{5,4},{6,7},{7,6},{8,9},{9,8},{10,11... | collective-permute-start | bytes 1585160 | tf_op jit(solution)/shard_map/ppermute | solution.py:149
  57.4 2.4 %collective-permute-done.8 = s32[128]{0:T(128)S(1)} collective-permute-done((s32[128]{0:T(128)S(1)}, s32[128]{0:T(128)S(1)}, u32[]{:S(2)}, u32[]{:S(2)}) %collective-permute-start.8) | collective-permute-done | bytes 544 | tf_op jit(solution)/shard_map/ppermute | solution.py:149
  59.8 1.9 %collective-permute-start.3 = (bf16[2064,128]{1,0:T(8,128)(2,1)S(1)}, bf16[2064,128]{1,0:T(8,128)(2,1)}, u32[]{:S(2)}, u32[]{:S(2)}) collective-permute-start(bf16[2064,128]{1,0:T(8,128)(2,1)S(1)} %collective-permute-done.1.refs_2_), channel_id=1, source_target_pairs={{0,1},{1,0},{2,3},{3,2},{4,5},{5,4},{6,7},{7,6},{8,9},{9,8},{10,11... | collective-permute-start | bytes 1585160 | tf_op jit(solution)/shard_map/ppermute | solution.py:149
  61.7 0.0 collective-permute-done.5.refs_6_
  61.7 2.4 %collective-permute-start.6 = (bf16[2064,128]{1,0:T(8,128)(2,1)S(1)}, bf16[2064,128]{1,0:T(8,128)(2,1)}, u32[]{:S(2)}, u32[]{:S(2)}) collective-permute-start(bf16[2064,128]{1,0:T(8,128)(2,1)S(1)} %collective-permute-done.5.refs_6_), channel_id=1, source_target_pairs={{0,1},{1,0},{2,3},{3,2},{4,5},{5,4},{6,7},{7,6},{8,9},{9,8},{10,11... | collective-permute-start | bytes 1585160 | tf_op jit(solution)/shard_map/ppermute | solution.py:149
  64.1 0.1 sub.25
  64.2 0.0 copy-done
  64.2 0.1 pad_add_fusion.params
  64.3 9.2 %psum.30 = s32[128]{0:T(128)S(1)} all-reduce(s32[128]{0:T(128)S(1)} %broadcast_select_fusion), channel_id=1, replica_groups=mesh['row'=32,'x'=4,'y'=4,'core'=2] {'y','core'}, use_global_device_ids=true, to_apply=%region_4.5 | all-reduce | flops 128 | bytes 1024 | tf_op jit(solution)/shard_map/psum | solution.py:169
  73.5 19.1 %psum.31 = s32[128]{0:T(128)S(1)} all-reduce(s32[128]{0:T(128)S(1)} %psum.30), channel_id=1, replica_groups=mesh['row'=32,'x'=4,'y'=4,'core'=2] {'x'}, use_global_device_ids=true, to_apply=%region_5.6 | all-reduce | flops 128 | bytes 1024 | tf_op jit(solution)/shard_map/psum | solution.py:170
  93.3 0.0 collective-permute-done.refs_1_
  93.3 0.0 collective-permute-done.7.refs_8_
  93.3 0.0 collective-permute-done.4.refs_5_
  93.3 0.0 collective-permute-done.3.refs_4_
  93.3 0.0 collective-permute-done.6.refs_7_
  93.3 8.7 %products.1 = bf16[66,128,128]{2,1,0:T(8,128)(2,1)} custom-call(s32[104]{0:T(128)S(1)} %pad_add_fusion.params, bf16[2064,128]{1,0:T(8,128)(2,1)S(1)} %fusion.1.refs_0_, bf16[2064,128]{1,0:T(8,128)(2,1)S(1)} %collective-permute-done.refs_1_, bf16[2064,128]{1,0:T(8,128)(2,1)S(1)} %collective-permute-done.1.refs_2_, ...), custom_call_target="tpu_custom_call" | custom-call | flops 600000000 | bytes 8000000 | tf_op jit(solution)/shard_map/products/pallas_call | solution.py:108
  (6 shorter events, 0.0 us)
Async XLA Ops:
  0.6 63.6 %copy-start = (s32[1,1,66]{2,1,0:T(1,128)S(1)}, s32[1,1,66]{2,1,0:T(1,128)}, u32[]{:S(2)}) copy-start(s32[1,1,66]{2,1,0:T(1,128)} %param.7) | copy-start | bytes 796
  2.5 41.6 %collective-permute-start.1 = (bf16[2064,128]{1,0:T(8,128)(2,1)S(1)}, bf16[2064,128]{1,0:T(8,128)(2,1)S(1)}, u32[]{:S(2)}, u32[]{:S(2)}) collective-permute-start(bf16[2064,128]{1,0:T(8,128)(2,1)S(1)} %fusion.1.refs_0_), channel_id=1, source_target_pairs={{0,1022},{1,3},{2,0},{3,5},{4,2},{5,7},{6,4},{7,9},{8,6},{9,11},{1... | collective-permute-start | bytes 1585160 | tf_op jit(solution)/shard_map/ppermute | solution.py:149
  5.2 44.3 %collective-permute-start.2 = (bf16[2064,128]{1,0:T(8,128)(2,1)S(1)}, bf16[2064,128]{1,0:T(8,128)(2,1)S(1)}, u32[]{:S(2)}, u32[]{:S(2)}) collective-permute-start(bf16[2064,128]{1,0:T(8,128)(2,1)S(1)} %fusion.1.refs_0_), channel_id=1, source_target_pairs={{0,2},{1,1023},{2,4},{3,1},{4,6},{5,3},{6,8},{7,5},{8,10},{9,7},{1... | collective-permute-start | bytes 1585160 | tf_op jit(solution)/shard_map/ppermute | solution.py:149
  10.5 82.8 %collective-permute-start = (bf16[2064,128]{1,0:T(8,128)(2,1)S(1)}, bf16[2064,128]{1,0:T(8,128)(2,1)S(1)}, u32[]{:S(2)}, u32[]{:S(2)}) collective-permute-start(bf16[2064,128]{1,0:T(8,128)(2,1)S(1)} %fusion.1.refs_0_), channel_id=1, source_target_pairs={{0,1},{1,0},{2,3},{3,2},{4,5},{5,4},{6,7},{7,6},{8,9},{9,8},{10,11... | collective-permute-start | bytes 1585160 | tf_op jit(solution)/shard_map/ppermute | solution.py:149
  44.1 17.6 %collective-permute-start.5 = (bf16[2064,128]{1,0:T(8,128)(2,1)S(1)}, bf16[2064,128]{1,0:T(8,128)(2,1)S(1)}, u32[]{:S(2)}, u32[]{:S(2)}) collective-permute-start(bf16[2064,128]{1,0:T(8,128)(2,1)S(1)} %collective-permute-done.1.refs_2_), channel_id=1, source_target_pairs={{0,1022},{1,3},{2,0},{3,5},{4,2},{5,7},{6,4},{7,9},{8,6},{9,11},{1... | collective-permute-start | bytes 1585160 | tf_op jit(solution)/shard_map/ppermute | solution.py:149
  47.4 12.4 %collective-permute-start.8 = (s32[128]{0:T(128)S(1)}, s32[128]{0:T(128)S(1)}, u32[]{:S(2)}, u32[]{:S(2)}) collective-permute-start(s32[128]{0:T(128)S(1)} %broadcast_in_dim.36), channel_id=1, source_target_pairs={{1,33},{2,66},{3,99},{4,132},{5,165},{6,198},{7,231},{8,264},{9,29... | collective-permute-start | bytes 1544 | tf_op jit(solution)/shard_map/ppermute | solution.py:149
  49.4 43.9 %collective-permute-start.7 = (bf16[2064,128]{1,0:T(8,128)(2,1)S(1)}, bf16[2064,128]{1,0:T(8,128)(2,1)S(1)}, u32[]{:S(2)}, u32[]{:S(2)}) collective-permute-start(bf16[2064,128]{1,0:T(8,128)(2,1)S(1)} %collective-permute-done.2.refs_3_), channel_id=1, source_target_pairs={{0,2},{1,1023},{2,4},{3,1},{4,6},{5,3},{6,8},{7,5},{8,10},{9,7},{1... | collective-permute-start | bytes 1585160 | tf_op jit(solution)/shard_map/ppermute | solution.py:149
  55.5 37.8 %collective-permute-start.4 = (bf16[2064,128]{1,0:T(8,128)(2,1)S(1)}, bf16[2064,128]{1,0:T(8,128)(2,1)}, u32[]{:S(2)}, u32[]{:S(2)}) collective-permute-start(bf16[2064,128]{1,0:T(8,128)(2,1)S(1)} %collective-permute-done.2.refs_3_), channel_id=1, source_target_pairs={{0,1},{1,0},{2,3},{3,2},{4,5},{5,4},{6,7},{7,6},{8,9},{9,8},{10,11... | collective-permute-start | bytes 1585160 | tf_op jit(solution)/shard_map/ppermute | solution.py:149
  59.8 33.5 %collective-permute-start.3 = (bf16[2064,128]{1,0:T(8,128)(2,1)S(1)}, bf16[2064,128]{1,0:T(8,128)(2,1)}, u32[]{:S(2)}, u32[]{:S(2)}) collective-permute-start(bf16[2064,128]{1,0:T(8,128)(2,1)S(1)} %collective-permute-done.1.refs_2_), channel_id=1, source_target_pairs={{0,1},{1,0},{2,3},{3,2},{4,5},{5,4},{6,7},{7,6},{8,9},{9,8},{10,11... | collective-permute-start | bytes 1585160 | tf_op jit(solution)/shard_map/ppermute | solution.py:149
  61.7 31.6 %collective-permute-start.6 = (bf16[2064,128]{1,0:T(8,128)(2,1)S(1)}, bf16[2064,128]{1,0:T(8,128)(2,1)}, u32[]{:S(2)}, u32[]{:S(2)}) collective-permute-start(bf16[2064,128]{1,0:T(8,128)(2,1)S(1)} %collective-permute-done.5.refs_6_), channel_id=1, source_target_pairs={{0,1},{1,0},{2,3},{3,2},{4,5},{5,4},{6,7},{7,6},{8,9},{9,8},{10,11... | collective-permute-start | bytes 1585160 | tf_op jit(solution)/shard_map/ppermute | solution.py:149
